TPU v7x, 256 devices: a whole 4x4x8 slice. The times are simulated.
256 devices in a mesh: blk: 128 (over z, y, x_hi, core), rep: 2 (over x_lo).
Axes of the slice: x: 4 (x_hi: 2, x_lo: 2; x = x_hi * 2 + x_lo), y: 4, z: 8, core: 2. Of those that a mesh axis runs over, the one named last changes fastest.
Arguments:
- inputs: bfloat16 [32768, 5120], P(('blk', 'rep')), may hold values from -6 to 6
- upstream: bfloat16 [32768, 5120], P(('blk', 'rep')), may hold values from -6 to 6
- w_gate_t: bfloat16 [27648, 5120], P('blk', 'rep'), may hold values from -0.078125 to 0.078125
- w_up_t: bfloat16 [27648, 5120], P('blk', 'rep'), may hold values from -0.078125 to 0.078125
- w_down: bfloat16 [27648, 5120], P('blk', 'rep'), may hold values from -0.3125 to 0.3125
Outputs:
- grad_inputs: bfloat16 [32768, 5120], P(('blk', 'rep'))
- grad_gate_t: bfloat16 [27648, 5120], P('blk', 'rep')
- grad_up_t: bfloat16 [27648, 5120], P('blk', 'rep')
- grad_down: bfloat16 [27648, 5120], P('blk', 'rep')
All inputs are finite; a program needn't handle non-finite values.
Results may differ from a plain program's by a relative error of at most 0.0049.
Values may be sent and summed in bfloat16 or wider, within the bound.
No kernel may reach another device: no remote copies, remote signals or barrier semaphores. Data moves between devices by JAX's collectives and lax.ppermute only.
A program may use at most 128 MiB of HBM per device.

v0:
```python
import functools

import jax
import jax.numpy as jnp
from jax import lax
from jax.experimental import pallas as pl
from jax.experimental.pallas import tpu as pltpu
from jax.sharding import PartitionSpec as P

BF = jnp.bfloat16
F32 = jnp.float32
AXES = ("blk", "rep")
LAST = (((1,), (1,)), ((), ()))
IN_VMEM = pl.BlockSpec(memory_space=pltpu.VMEM)
IN_SMEM = pl.BlockSpec(memory_space=pltpu.SMEM)


def routes(n_blk):
    def at(b, r):
        return (b % n_blk) * 2 + r

    every = [(b, r) for b in range(n_blk) for r in (0, 1)]
    return {
        "swap": [(at(b, r), at(b, 1 - r)) for b, r in every],
        "back": [(at(b, r), at(b - 1, r)) for b, r in every],
        "back_flip": [(at(b, r), at(b - 1, r if b % 2 else 1 - r)) for b, r in every],
        "same_chip": [(at(b, r), at(b ^ 1, r)) for b, r in every],
        "fwd": [(at(b, r), at(b + 1, r)) for b, r in every],
        "fwd_flip": [(at(b, r), at(b + 1, 1 - r if b % 2 else r)) for b, r in every],
        "swap_even": [(at(b, r), at(b, 1 - r)) for b, r in every if b % 2 == 0],
        "swap_odd": [(at(b, r), at(b, 1 - r)) for b, r in every if b % 2 == 1],
    }


def call(body, args, outs, flops, scratch=(), scalars=0):
    shapes = [jax.ShapeDtypeStruct(s, t) for s, t in outs]
    nbytes = sum(a.size * a.dtype.itemsize for a in (*args, *shapes))
    return pl.pallas_call(
        body,
        in_specs=[IN_SMEM] * scalars + [IN_VMEM] * (len(args) - scalars),
        out_specs=[IN_VMEM] * len(shapes),
        out_shape=shapes,
        scratch_shapes=list(scratch),
        compiler_params=pltpu.CompilerParams(vmem_limit_bytes=nbytes + (4 << 20)),
        cost_estimate=pl.CostEstimate(flops=flops, bytes_accessed=nbytes, transcendentals=0),
    )(*args)


def pre1_body(t, wg, wu, wd, out, out16):
    rows = t.shape[0] // 2
    x, g = t[:rows], t[rows:]
    for i, (w, v) in enumerate(((wg, x), (wu, x), (wd, g))):
        s = lax.dot_general(w[...], v, LAST, preferred_element_type=F32)
        out[i] = s
        out16[i] = s.astype(BF)


def pre1(tokens, weights):
    rows, width = tokens.shape
    hid = weights[0].shape[0]
    shape = (3, hid, rows // 2)
    return call(
        pre1_body, (tokens, *weights), [(shape, F32), (shape, BF)], 3 * rows * width * hid
    )


def pre2_body(odd, own, by_link, by_chip, wg, wu, wd, out, out16, oth):
    rows = own.shape[0] // 2

    @pl.when(odd[0] == 1)
    def _():
        oth[...] = by_link[...]

    @pl.when(odd[0] == 0)
    def _():
        oth[...] = by_chip[...]

    x = jnp.concatenate([own[:rows], oth[:rows]], 0)
    g = jnp.concatenate([own[rows:], oth[rows:]], 0)
    for i, (w, t) in enumerate(((wg, x), (wu, x), (wd, g))):
        s = lax.dot_general(w[...], t, LAST, preferred_element_type=F32)
        out[i] = s
        out16[i, :, :rows] = s[:, rows:].astype(BF)
        out16[i, :, rows:] = s[:, :rows].astype(BF)


def pre2(odd, own, by_link, by_chip, weights):
    rows, width = own.shape
    hid = weights[0].shape[0]
    shape = (3, hid, rows)
    return call(
        pre2_body,
        (odd, own, by_link, by_chip, *weights),
        [(shape, F32), (shape, BF), ((rows, width), BF)],
        6 * rows * width * hid,
        scalars=1,
    )


def act_body(pieces, chunks, *refs):
    ps, rs = refs[:pieces], refs[pieces : 2 * pieces]
    wg, wu, d = refs[2 * pieces : 2 * pieces + 3]
    own, oth, *more = refs[2 * pieces + 3 : -1]
    turned = refs[-1]
    at = 0
    for p, r in zip(ps, rs):
        gate = p[0] + r[0].astype(F32)
        up = p[1] + r[1].astype(F32)
        ga = p[2] + r[2].astype(F32)
        sig = 1.0 / (1.0 + jnp.exp(-gate))
        silu = gate * sig
        dgate = ga * up * sig * (1.0 + gate * (1.0 - sig))
        dup = ga * silu
        part = pl.ds(at, p.shape[2])
        d[0, :, part] = (silu * up).astype(BF)
        d[1, :, part] = dgate.astype(BF)
        d[2, :, part] = dup.astype(BF)
        turned[0, part, :] = dgate.T.astype(BF)
        turned[1, part, :] = dup.T.astype(BF)
        at += p.shape[2]
    rows, width = own.shape
    n = width // chunks

    @pl.loop(0, chunks)
    def _(c):
        cols = pl.ds(pl.multiple_of(c * n, n), n)
        s = jnp.dot(turned[0], wg[:, cols], preferred_element_type=F32)
        s += jnp.dot(turned[1], wu[:, cols], preferred_element_type=F32)
        own[:, cols] = s[:rows].astype(own.dtype)
        oth[:, cols] = s[rows:].astype(oth.dtype)
        for m in more:
            m[:, cols] = s[rows:].astype(m.dtype)


def act(ps, rs, wg, wu, kinds):
    hid, width = wg.shape
    total = sum(p.shape[2] for p in ps)
    rows = total // 2
    return call(
        functools.partial(act_body, len(ps), 5),
        (*ps, *rs, wg, wu),
        [((3, hid, total), BF)] + [((rows, width), t) for t in kinds],
        8 * rows * hid * width,
        scratch=[pltpu.VMEM((2, total, hid), BF)],
    )


def dw_body(chunks, d1, d2, *refs):
    tokens, outs = refs[:4], refs[4:]
    n = outs[0].shape[1] // chunks
    rows = tokens[0].shape[0] // 2

    @pl.loop(0, chunks)
    def _(c):
        cols = pl.ds(pl.multiple_of(c * n, n), n)
        x = jnp.concatenate([r[:rows, cols] for r in tokens], 0)
        g = jnp.concatenate([r[rows:, cols] for r in tokens], 0)
        for i, out, t in ((1, outs[0], x), (2, outs[1], x), (0, outs[2], g)):
            d = jnp.concatenate([d1[i], d2[i]], 1)
            out[:, cols] = jnp.dot(d, t, preferred_element_type=F32).astype(BF)


def dw(d1, d2, tokens):
    hid = d1.shape[1]
    rows, width = tokens[0].shape
    return call(
        functools.partial(dw_body, 5),
        (d1, d2, *tokens),
        [((hid, width), BF)] * 3,
        12 * rows * hid * width,
    )


def add_body(a, b, out):
    out[...] = (a[...] + b[...].astype(F32)).astype(BF)


def last_body(where, own1, own2, left, flip, s, out):
    half = own1.shape[1]
    own = pl.ds(pl.multiple_of(where[1] * half, 128), half)
    oth = pl.ds(pl.multiple_of((1 - where[1]) * half, 128), half)
    out[:, own] = (own1[...] + own2[...].astype(F32)).astype(BF)

    @pl.when(where[0] == 1)
    def _():
        out[:, oth] = s[...]

    @pl.when(where[0] == 0)
    def _():
        out[:, oth] = (left[...].astype(F32) + flip[...].astype(F32)).astype(BF)


def solution(mesh):
    route = routes(mesh.shape["blk"])

    def go(value, name):
        return lax.ppermute(value, AXES, route[name])

    def steps(inputs, upstream, w_gate_t, w_up_t, w_down):
        rows, width = inputs.shape
        half = width // 2
        weights = (w_gate_t, w_up_t, w_down)
        rep = lax.axis_index("rep").astype(jnp.int32)
        odd = (lax.axis_index("blk") % 2).astype(jnp.int32)

        def cut(a, b, at):
            return jnp.concatenate([lax.dynamic_slice(v, (0, at), (rows, half)) for v in (a, b)], 0)

        mine = cut(*lax.optimization_barrier((inputs, upstream)), rep * half)
        send = cut(inputs, upstream, (1 - rep) * half)
        theirs = go(send, "swap")
        by_link = go(send, "back_flip")
        p1_own, p1_own16 = pre1(mine, weights)
        r1_oth = go(p1_own16, "swap")
        mine2 = go(mine, "back")
        p1_oth, p1_oth16 = pre1(theirs, weights)
        r1_own = go(p1_oth16, "swap")
        by_chip = go(theirs, "same_chip")
        d1, own1, oth1_16, oth1 = act(
            (p1_own, p1_oth), (r1_own, r1_oth), w_gate_t, w_up_t, (F32, BF, F32)
        )
        left = go(oth1_16, "swap_even")
        p2, p2_16, theirs2 = pre2(odd.reshape(1), mine2, by_link, by_chip, weights)
        r2 = go(p2_16, "swap")
        d2, own2, oth2 = act((p2,), (r2,), w_gate_t, w_up_t, (BF, BF))
        oth2_chip = go(oth2, "same_chip")
        own2_home = go(own2, "fwd")
        flip = go(oth2, "fwd_flip")
        (s,) = call(add_body, (oth1, oth2_chip), [((rows, half), BF)], rows * half)
        s_odd = go(s, "swap_odd")
        gg, gu, gd = dw(d1, d2, (mine, theirs, mine2, theirs2))
        (d_in,) = call(
            last_body,
            (jnp.stack([odd, rep]), own1, own2_home, left, flip, s_odd),
            [((rows, width), BF)],
            2 * rows * width,
            scalars=1,
        )
        return d_in, gg, gu, gd

    tokens, weights = P(AXES, None), P("blk", "rep")
    return jax.shard_map(
        steps,
        mesh=mesh,
        in_specs=(tokens, tokens, weights, weights, weights),
        out_specs=(tokens, weights, weights, weights),
        check_vma=False,
    )
```

profile of v0, /device:TPU:1, one launch (start us, length us, event | category | flops | bytes accessed | tf_op | source)
XLA Modules:
  0.0 108.1 jit_solution(4218633666536085276)
XLA Ops:
  0.6 1.4 %constant_dynamic-slice_fusion = (bf16[128,2560]{1,0:T(8,128)(2,1)S(1)}, bf16[128,2560]{1,0:T(8,128)(2,1)S(1)}) fusion(bf16[128,5120]{1,0:T(8,128)(2,1)} %param.6, s32[]{:T(128)S(6)} %select_n.17, bf16[128,5120]{1,0:T(8,128)(2,1)} %param.5), kind=kLoop, calls=%fused_computation.2 | loop fusion | bytes 2621444 | tf_op jit(solution)/shard_map/dynamic_slice | solution.py:207
  2.0 0.0 copy-start.3
  2.0 1.2 %pad_maximum_fusion.1 = bf16[256,2560]{1,0:T(8,128)(2,1)} fusion(bf16[128,2560]{1,0:T(8,128)(2,1)S(1)} %get-tuple-element.44, bf16[128,2560]{1,0:T(8,128)(2,1)S(1)} %get-tuple-element.45), kind=kLoop, calls=%fused_computation.1 | loop fusion | flops 2621440 | bytes 2621440 | tf_op jit(solution)/shard_map/concatenate | solution.py:207
  3.2 2.0 %collective-permute-start = (bf16[256,2560]{1,0:T(8,128)(2,1)}, bf16[256,2560]{1,0:T(8,128)(2,1)}, u32[]{:S(2)}, u32[]{:S(2)}) collective-permute-start(bf16[256,2560]{1,0:T(8,128)(2,1)} %pad_maximum_fusion.1), channel_id=1, source_target_pairs={{0,1},{1,0},{2,3},{3,2},{4,5},{5,4},{6,7},{7,6},{8,9},{9,8},{10,11... | collective-permute-start | bytes 3932168 | tf_op jit(solution)/shard_map/ppermute | solution.py:197
  5.2 1.2 %collective-permute-start.4 = (bf16[256,2560]{1,0:T(8,128)(2,1)}, bf16[256,2560]{1,0:T(8,128)(2,1)}, u32[]{:S(2)}, u32[]{:S(2)}) collective-permute-start(bf16[256,2560]{1,0:T(8,128)(2,1)} %pad_maximum_fusion.1), channel_id=1, source_target_pairs={{0,255},{1,254},{2,0},{3,1},{4,3},{5,2},{6,4},{7,5},{8,7},{9,6},{1... | collective-permute-start | bytes 3932168 | tf_op jit(solution)/shard_map/ppermute | solution.py:197
  6.4 0.0 copy-done.3
  6.4 0.0 copy-start.2
  6.4 1.3 %constant_dynamic-slice_fusion.2 = (bf16[128,2560]{1,0:T(8,128)(2,1)S(1)}, bf16[128,2560]{1,0:T(8,128)(2,1)S(1)}) fusion(bf16[128,5120]{1,0:T(8,128)(2,1)S(1)} %copy-done.3, s32[]{:T(128)S(6)} %select_n.16, bf16[128,5120]{1,0:T(8,128)(2,1)} %param.5), kind=kLoop, calls=%fused_computation.4 | loop fusion | bytes 2621444 | tf_op jit(solution)/shard_map/dynamic_slice | solution.py:207
  7.7 0.0 copy-start
  7.7 0.0 copy-start.1
  7.7 1.1 %pad_maximum_fusion.t.refs_0_ = bf16[256,2560]{1,0:T(8,128)(2,1)} fusion(bf16[128,2560]{1,0:T(8,128)(2,1)S(1)} %get-tuple-element.42, bf16[128,2560]{1,0:T(8,128)(2,1)S(1)} %get-tuple-element.43), kind=kLoop, calls=%fused_computation | loop fusion | flops 2621440 | bytes 2621440 | tf_op jit(solution)/shard_map/concatenate | solution.py:207
  8.8 8.8 %collective-permute-start.3 = (bf16[256,2560]{1,0:T(8,128)(2,1)}, bf16[256,2560]{1,0:T(8,128)(2,1)}, u32[]{:S(2)}, u32[]{:S(2)}) collective-permute-start(bf16[256,2560]{1,0:T(8,128)(2,1)} %pad_maximum_fusion.t.refs_0_), channel_id=1, source_target_pairs={{0,254},{1,255},{2,0},{3,1},{4,2},{5,3},{6,4},{7,5},{8,6},{9,7},{1... | collective-permute-start | bytes 3932168 | tf_op jit(solution)/shard_map/ppermute | solution.py:197
  17.6 29.2 %collective-permute-done.t.refs_1_ = bf16[256,2560]{1,0:T(8,128)(2,1)} collective-permute-done((bf16[256,2560]{1,0:T(8,128)(2,1)}, bf16[256,2560]{1,0:T(8,128)(2,1)}, u32[]{:S(2)}, u32[]{:S(2)}) %collective-permute-start) | collective-permute-done | bytes 1310752 | tf_op jit(solution)/shard_map/ppermute | solution.py:197
  46.8 2.5 %collective-permute-start.5 = (bf16[256,2560]{1,0:T(8,128)(2,1)}, bf16[256,2560]{1,0:T(8,128)(2,1)}, u32[]{:S(2)}, u32[]{:S(2)}) collective-permute-start(bf16[256,2560]{1,0:T(8,128)(2,1)} %collective-permute-done.t.refs_1_), channel_id=1, source_target_pairs={{0,2},{1,3},{2,0},{3,1},{4,6},{5,7},{6,4},{7,5},{8,10},{9,11},{10,... | collective-permute-start | bytes 3932168 | tf_op jit(solution)/shard_map/ppermute | solution.py:197
  49.3 1.8 %collective-permute-done.3.own.refs_2_ = bf16[256,2560]{1,0:T(8,128)(2,1)} collective-permute-done((bf16[256,2560]{1,0:T(8,128)(2,1)}, bf16[256,2560]{1,0:T(8,128)(2,1)}, u32[]{:S(2)}, u32[]{:S(2)}) %collective-permute-start.3) | collective-permute-done | bytes 1310752 | tf_op jit(solution)/shard_map/ppermute | solution.py:197
  51.1 0.0 collective-permute-done.4.by_link
  51.1 1.2 %collective-permute-done.5.by_chip = bf16[256,2560]{1,0:T(8,128)(2,1)} collective-permute-done((bf16[256,2560]{1,0:T(8,128)(2,1)}, bf16[256,2560]{1,0:T(8,128)(2,1)}, u32[]{:S(2)}, u32[]{:S(2)}) %collective-permute-start.5) | collective-permute-done | bytes 1310752 | tf_op jit(solution)/shard_map/ppermute | solution.py:197
  52.3 0.0 copy-done.2
  52.3 0.0 copy-done
  52.3 0.0 copy-done.1
  52.3 3.5 %shard_map.87 = (f32[3,216,256]{2,1,0:T(8,128)S(1)}, bf16[3,216,256]{2,1,0:T(8,128)(2,1)S(1)}, bf16[256,2560]{1,0:T(8,128)(2,1)S(1)}) custom-call(s32[1]{0:T(128)} %bitcast.odd, bf16[256,2560]{1,0:T(8,128)(2,1)} %collective-permute-done.3.own.refs_2_, bf16[256,2560]{1,0:T(8,128)(2,1)} %collective-permute-done.4.by_link, ...), custom_call_target="tpu_custom_call" | custom-call | flops 849346560 | bytes 9555972 | tf_op jit(solution)/shard_map/pallas_call | solution.py:38
  55.8 1.5 %collective-permute-start.6 = (bf16[3,216,256]{2,1,0:T(8,128)(2,1)S(1)}, bf16[3,216,256]{2,1,0:T(8,128)(2,1)S(1)}, u32[]{:S(2)}, u32[]{:S(2)}) collective-permute-start(bf16[3,216,256]{2,1,0:T(8,128)(2,1)S(1)} %get-tuple-element.31), channel_id=1, source_target_pairs={{0,1},{1,0},{2,3},{3,2},{4,5},{5,4},{6,7},{7,6},{8,9},{9,8},{10,11... | collective-permute-start | bytes 995336 | tf_op jit(solution)/shard_map/ppermute | solution.py:197
  57.4 7.5 %collective-permute-done.6.refs_1_ = bf16[3,216,256]{2,1,0:T(8,128)(2,1)S(1)} collective-permute-done((bf16[3,216,256]{2,1,0:T(8,128)(2,1)S(1)}, bf16[3,216,256]{2,1,0:T(8,128)(2,1)S(1)}, u32[]{:S(2)}, u32[]{:S(2)}) %collective-permute-start.6) | collective-permute-done | bytes 331808 | tf_op jit(solution)/shard_map/ppermute | solution.py:197
  64.9 1.7 %shard_map.88 = (bf16[3,216,256]{2,1,0:T(8,128)(2,1)S(1)}, bf16[128,2560]{1,0:T(8,128)(2,1)S(1)}, bf16[128,2560]{1,0:T(8,128)(2,1)S(1)}) custom-call(f32[3,216,256]{2,1,0:T(8,128)S(1)} %get-tuple-element.30.refs_0_, bf16[3,216,256]{2,1,0:T(8,128)(2,1)S(1)} %collective-permute-done.6.refs_1_, bf16[216,2560]{1,0:T(8,128)(2,1)S(1)} %copy-done, ...), custom_call_target="tpu_custom_call" | custom-call | flops 566231040 | bytes 4849664 | tf_op jit(solution)/shard_map/pallas_call | solution.py:38
  66.6 1.3 %collective-permute-start.10 = (bf16[128,2560]{1,0:T(8,128)(2,1)S(1)}, bf16[128,2560]{1,0:T(8,128)(2,1)S(1)}, u32[]{:S(2)}, u32[]{:S(2)}) collective-permute-start(bf16[128,2560]{1,0:T(8,128)(2,1)S(1)} %get-tuple-element.34), channel_id=1, source_target_pairs={{0,2},{1,3},{2,0},{3,1},{4,6},{5,7},{6,4},{7,5},{8,10},{9,11},{10,... | collective-permute-start | bytes 1966088 | tf_op jit(solution)/shard_map/ppermute | solution.py:197
  68.0 2.4 %shard_map.84 = (f32[3,216,128]{2,1,0:T(8,128)S(1)}, bf16[3,216,128]{2,1,0:T(8,128)(2,1)S(1)}) custom-call(bf16[256,2560]{1,0:T(8,128)(2,1)} %pad_maximum_fusion.t.refs_0_, bf16[216,2560]{1,0:T(8,128)(2,1)S(1)} %copy-done, bf16[216,2560]{1,0:T(8,128)(2,1)S(1)} %copy-done.1, bf16[216,2560]{1,0:T(8,128)(2,1)S(1)} %copy-done.2), custom_call_target="tpu_custom_call" | custom-call | flops 424673280 | bytes 5126144 | tf_op jit(solution)/shard_map/pallas_call | solution.py:38
  70.3 1.5 %collective-permute-start.2 = (bf16[3,216,128]{2,1,0:T(8,128)(2,1)S(1)}, bf16[3,216,128]{2,1,0:T(8,128)(2,1)S(1)}, u32[]{:S(2)}, u32[]{:S(2)}) collective-permute-start(bf16[3,216,128]{2,1,0:T(8,128)(2,1)S(1)} %get-tuple-element.28), channel_id=1, source_target_pairs={{0,1},{1,0},{2,3},{3,2},{4,5},{5,4},{6,7},{7,6},{8,9},{9,8},{10,11... | collective-permute-start | bytes 497672 | tf_op jit(solution)/shard_map/ppermute | solution.py:197
  71.9 2.4 %shard_map.85 = (f32[3,216,128]{2,1,0:T(8,128)S(1)}, bf16[3,216,128]{2,1,0:T(8,128)(2,1)S(1)}) custom-call(bf16[256,2560]{1,0:T(8,128)(2,1)} %collective-permute-done.t.refs_1_, bf16[216,2560]{1,0:T(8,128)(2,1)S(1)} %copy-done, bf16[216,2560]{1,0:T(8,128)(2,1)S(1)} %copy-done.1, bf16[216,2560]{1,0:T(8,128)(2,1)S(1)} %copy-done.2), custom_call_target="tpu_custom_call" | custom-call | flops 424673280 | bytes 5126144 | tf_op jit(solution)/shard_map/pallas_call | solution.py:38
  74.2 0.1 collective-permute-start.1
  74.3 1.9 %collective-permute-done.2.refs_3_ = bf16[3,216,128]{2,1,0:T(8,128)(2,1)S(1)} collective-permute-done((bf16[3,216,128]{2,1,0:T(8,128)(2,1)S(1)}, bf16[3,216,128]{2,1,0:T(8,128)(2,1)S(1)}, u32[]{:S(2)}, u32[]{:S(2)}) %collective-permute-start.2) | collective-permute-done | bytes 165920 | tf_op jit(solution)/shard_map/ppermute | solution.py:197
  76.2 3.6 %collective-permute-done.1.refs_2_ = bf16[3,216,128]{2,1,0:T(8,128)(2,1)S(1)} collective-permute-done((bf16[3,216,128]{2,1,0:T(8,128)(2,1)S(1)}, bf16[3,216,128]{2,1,0:T(8,128)(2,1)S(1)}, u32[]{:S(2)}, u32[]{:S(2)}) %collective-permute-start.1) | collective-permute-done | bytes 165920 | tf_op jit(solution)/shard_map/ppermute | solution.py:197
  79.8 1.7 %shard_map.86 = (bf16[3,216,256]{2,1,0:T(8,128)(2,1)S(1)}, f32[128,2560]{1,0:T(8,128)S(1)}, bf16[128,2560]{1,0:T(8,128)(2,1)S(1)}, f32[128,2560]{1,0:T(8,128)S(1)}) custom-call(f32[3,216,128]{2,1,0:T(8,128)S(1)} %get-tuple-element.25.refs_0_, f32[3,216,128]{2,1,0:T(8,128)S(1)} %get-tuple-element.26.refs_1_, ...), custom_call_target="tpu_custom_call" | custom-call | flops 566231040 | bytes 6815744 | tf_op jit(solution)/shard_map/pallas_call | solution.py:38
  81.6 0.7 collective-permute-start.8
  82.3 1.1 collective-permute-start.9
  83.3 0.4 collective-permute-start.7
  83.7 0.0 collective-permute-done.10.b
  83.7 0.1 shard_map.89
  83.8 2.2 %collective-permute-start.11 = (bf16[128,2560]{1,0:T(8,128)(2,1)S(1)}, bf16[128,2560]{1,0:T(8,128)(2,1)S(1)}, u32[]{:S(2)}, u32[]{:S(2)}) collective-permute-start(bf16[128,2560]{1,0:T(8,128)(2,1)S(1)} %shard_map.89), channel_id=1, source_target_pairs={{2,3},{3,2},{6,7},{7,6},{10,11},{11,10},{14,15},{15,14},{18,19},{1... | collective-permute-start | bytes 1966088 | tf_op jit(solution)/shard_map/ppermute | solution.py:197
  86.0 0.1 pad_add_fusion.where
  86.1 6.2 %shard_map.91 = (bf16[216,2560]{1,0:T(8,128)(2,1)}, bf16[216,2560]{1,0:T(8,128)(2,1)}, bf16[216,2560]{1,0:T(8,128)(2,1)}) custom-call(bf16[3,216,256]{2,1,0:T(8,128)(2,1)S(1)} %get-tuple-element.36.d1, bf16[3,216,256]{2,1,0:T(8,128)(2,1)S(1)} %get-tuple-element.37.d2, bf16[256,2560]{1,0:T(8,128)(2,1)} %pad_maximum_fusion.t.refs_0_, ...), custom_call_target="tpu_custom_call" | custom-call | flops 1698693120 | bytes 9224192 | tf_op jit(solution)/shard_map/pallas_call | solution.py:38
  92.3 0.0 collective-permute-done.8.left
  92.3 3.5 %collective-permute-done.7.own2 = bf16[128,2560]{1,0:T(8,128)(2,1)S(1)} collective-permute-done((bf16[128,2560]{1,0:T(8,128)(2,1)S(1)}, bf16[128,2560]{1,0:T(8,128)(2,1)S(1)}, u32[]{:S(2)}, u32[]{:S(2)}) %collective-permute-start.7) | collective-permute-done | bytes 655392 | tf_op jit(solution)/shard_map/ppermute | solution.py:197
  95.8 2.1 %collective-permute-done.9.flip = bf16[128,2560]{1,0:T(8,128)(2,1)S(1)} collective-permute-done((bf16[128,2560]{1,0:T(8,128)(2,1)S(1)}, bf16[128,2560]{1,0:T(8,128)(2,1)S(1)}, u32[]{:S(2)}, u32[]{:S(2)}) %collective-permute-start.9) | collective-permute-done | bytes 655392 | tf_op jit(solution)/shard_map/ppermute | solution.py:197
  97.9 8.5 %collective-permute-done.11.s = bf16[128,2560]{1,0:T(8,128)(2,1)S(1)} collective-permute-done((bf16[128,2560]{1,0:T(8,128)(2,1)S(1)}, bf16[128,2560]{1,0:T(8,128)(2,1)S(1)}, u32[]{:S(2)}, u32[]{:S(2)}) %collective-permute-start.11) | collective-permute-done | bytes 655392 | tf_op jit(solution)/shard_map/ppermute | solution.py:197
  106.4 1.8 %shard_map.90 = bf16[128,5120]{1,0:T(8,128)(2,1)} custom-call(s32[2]{0:T(128)S(1)} %pad_add_fusion.where, f32[128,2560]{1,0:T(8,128)S(1)} %get-tuple-element.29.own1, bf16[128,2560]{1,0:T(8,128)(2,1)S(1)} %collective-permute-done.7.own2, bf16[128,2560]{1,0:T(8,128)(2,1)S(1)} %collective-permute-done.8.left, ...), custom_call_target="tpu_custom_call" | custom-call | flops 1310720 | bytes 5242888 | tf_op jit(solution)/shard_map/pallas_call | solution.py:38
Async XLA Ops:
  2.0 4.4 %copy-start.3 = (bf16[128,5120]{1,0:T(8,128)(2,1)S(1)}, bf16[128,5120]{1,0:T(8,128)(2,1)}, u32[]{:S(2)}) copy-start(bf16[128,5120]{1,0:T(8,128)(2,1)} %param.6) | copy-start | bytes 3932164
  3.2 43.6 %collective-permute-start = (bf16[256,2560]{1,0:T(8,128)(2,1)}, bf16[256,2560]{1,0:T(8,128)(2,1)}, u32[]{:S(2)}, u32[]{:S(2)}) collective-permute-start(bf16[256,2560]{1,0:T(8,128)(2,1)} %pad_maximum_fusion.1), channel_id=1, source_target_pairs={{0,1},{1,0},{2,3},{3,2},{4,5},{5,4},{6,7},{7,6},{8,9},{9,8},{10,11... | collective-permute-start | bytes 3932168 | tf_op jit(solution)/shard_map/ppermute | solution.py:197
  5.2 45.8 %collective-permute-start.4 = (bf16[256,2560]{1,0:T(8,128)(2,1)}, bf16[256,2560]{1,0:T(8,128)(2,1)}, u32[]{:S(2)}, u32[]{:S(2)}) collective-permute-start(bf16[256,2560]{1,0:T(8,128)(2,1)} %pad_maximum_fusion.1), channel_id=1, source_target_pairs={{0,255},{1,254},{2,0},{3,1},{4,3},{5,2},{6,4},{7,5},{8,7},{9,6},{1... | collective-permute-start | bytes 3932168 | tf_op jit(solution)/shard_map/ppermute | solution.py:197
  6.4 45.9 %copy-start.2 = (bf16[216,2560]{1,0:T(8,128)(2,1)S(1)}, bf16[216,2560]{1,0:T(8,128)(2,1)}, u32[]{:S(2)}) copy-start(bf16[216,2560]{1,0:T(8,128)(2,1)} %wd.5) | copy-start | bytes 3317764
  7.7 44.6 %copy-start = (bf16[216,2560]{1,0:T(8,128)(2,1)S(1)}, bf16[216,2560]{1,0:T(8,128)(2,1)}, u32[]{:S(2)}) copy-start(bf16[216,2560]{1,0:T(8,128)(2,1)} %refs_2_.1) | copy-start | bytes 3317764
  7.7 44.6 %copy-start.1 = (bf16[216,2560]{1,0:T(8,128)(2,1)S(1)}, bf16[216,2560]{1,0:T(8,128)(2,1)}, u32[]{:S(2)}) copy-start(bf16[216,2560]{1,0:T(8,128)(2,1)} %refs_3_.1) | copy-start | bytes 3317764
  8.8 42.2 %collective-permute-start.3 = (bf16[256,2560]{1,0:T(8,128)(2,1)}, bf16[256,2560]{1,0:T(8,128)(2,1)}, u32[]{:S(2)}, u32[]{:S(2)}) collective-permute-start(bf16[256,2560]{1,0:T(8,128)(2,1)} %pad_maximum_fusion.t.refs_0_), channel_id=1, source_target_pairs={{0,254},{1,255},{2,0},{3,1},{4,2},{5,3},{6,4},{7,5},{8,6},{9,7},{1... | collective-permute-start | bytes 3932168 | tf_op jit(solution)/shard_map/ppermute | solution.py:197
  46.8 5.5 %collective-permute-start.5 = (bf16[256,2560]{1,0:T(8,128)(2,1)}, bf16[256,2560]{1,0:T(8,128)(2,1)}, u32[]{:S(2)}, u32[]{:S(2)}) collective-permute-start(bf16[256,2560]{1,0:T(8,128)(2,1)} %collective-permute-done.t.refs_1_), channel_id=1, source_target_pairs={{0,2},{1,3},{2,0},{3,1},{4,6},{5,7},{6,4},{7,5},{8,10},{9,11},{10,... | collective-permute-start | bytes 3932168 | tf_op jit(solution)/shard_map/ppermute | solution.py:197
  55.8 9.1 %collective-permute-start.6 = (bf16[3,216,256]{2,1,0:T(8,128)(2,1)S(1)}, bf16[3,216,256]{2,1,0:T(8,128)(2,1)S(1)}, u32[]{:S(2)}, u32[]{:S(2)}) collective-permute-start(bf16[3,216,256]{2,1,0:T(8,128)(2,1)S(1)} %get-tuple-element.31), channel_id=1, source_target_pairs={{0,1},{1,0},{2,3},{3,2},{4,5},{5,4},{6,7},{7,6},{8,9},{9,8},{10,11... | collective-permute-start | bytes 995336 | tf_op jit(solution)/shard_map/ppermute | solution.py:197
  66.6 17.0 %collective-permute-start.10 = (bf16[128,2560]{1,0:T(8,128)(2,1)S(1)}, bf16[128,2560]{1,0:T(8,128)(2,1)S(1)}, u32[]{:S(2)}, u32[]{:S(2)}) collective-permute-start(bf16[128,2560]{1,0:T(8,128)(2,1)S(1)} %get-tuple-element.34), channel_id=1, source_target_pairs={{0,2},{1,3},{2,0},{3,1},{4,6},{5,7},{6,4},{7,5},{8,10},{9,11},{10,... | collective-permute-start | bytes 1966088 | tf_op jit(solution)/shard_map/ppermute | solution.py:197
  70.3 5.9 %collective-permute-start.2 = (bf16[3,216,128]{2,1,0:T(8,128)(2,1)S(1)}, bf16[3,216,128]{2,1,0:T(8,128)(2,1)S(1)}, u32[]{:S(2)}, u32[]{:S(2)}) collective-permute-start(bf16[3,216,128]{2,1,0:T(8,128)(2,1)S(1)} %get-tuple-element.28), channel_id=1, source_target_pairs={{0,1},{1,0},{2,3},{3,2},{4,5},{5,4},{6,7},{7,6},{8,9},{9,8},{10,11... | collective-permute-start | bytes 497672 | tf_op jit(solution)/shard_map/ppermute | solution.py:197
  74.2 5.6 %collective-permute-start.1 = (bf16[3,216,128]{2,1,0:T(8,128)(2,1)S(1)}, bf16[3,216,128]{2,1,0:T(8,128)(2,1)S(1)}, u32[]{:S(2)}, u32[]{:S(2)}) collective-permute-start(bf16[3,216,128]{2,1,0:T(8,128)(2,1)S(1)} %get-tuple-element.27), channel_id=1, source_target_pairs={{0,1},{1,0},{2,3},{3,2},{4,5},{5,4},{6,7},{7,6},{8,9},{9,8},{10,11... | collective-permute-start | bytes 497672 | tf_op jit(solution)/shard_map/ppermute | solution.py:197
  81.6 10.8 %collective-permute-start.8 = (bf16[128,2560]{1,0:T(8,128)(2,1)S(1)}, bf16[128,2560]{1,0:T(8,128)(2,1)S(1)}, u32[]{:S(2)}, u32[]{:S(2)}) collective-permute-start(bf16[128,2560]{1,0:T(8,128)(2,1)S(1)} %get-tuple-element.33), channel_id=1, source_target_pairs={{0,1},{1,0},{4,5},{5,4},{8,9},{9,8},{12,13},{13,12},{16,17},{17,16... | collective-permute-start | bytes 1966088 | tf_op jit(solution)/shard_map/ppermute | solution.py:197
  82.3 15.6 %collective-permute-start.9 = (bf16[128,2560]{1,0:T(8,128)(2,1)S(1)}, bf16[128,2560]{1,0:T(8,128)(2,1)S(1)}, u32[]{:S(2)}, u32[]{:S(2)}) collective-permute-start(bf16[128,2560]{1,0:T(8,128)(2,1)S(1)} %get-tuple-element.34), channel_id=1, source_target_pairs={{0,2},{1,3},{2,5},{3,4},{4,6},{5,7},{6,9},{7,8},{8,10},{9,11},{10,... | collective-permute-start | bytes 1966088 | tf_op jit(solution)/shard_map/ppermute | solution.py:197
  83.3 12.5 %collective-permute-start.7 = (bf16[128,2560]{1,0:T(8,128)(2,1)S(1)}, bf16[128,2560]{1,0:T(8,128)(2,1)S(1)}, u32[]{:S(2)}, u32[]{:S(2)}) collective-permute-start(bf16[128,2560]{1,0:T(8,128)(2,1)S(1)} %get-tuple-element.32), channel_id=1, source_target_pairs={{0,2},{1,3},{2,4},{3,5},{4,6},{5,7},{6,8},{7,9},{8,10},{9,11},{10,... | collective-permute-start | bytes 1966088 | tf_op jit(solution)/shard_map/ppermute | solution.py:197
  83.8 22.5 %collective-permute-start.11 = (bf16[128,2560]{1,0:T(8,128)(2,1)S(1)}, bf16[128,2560]{1,0:T(8,128)(2,1)S(1)}, u32[]{:S(2)}, u32[]{:S(2)}) collective-permute-start(bf16[128,2560]{1,0:T(8,128)(2,1)S(1)} %shard_map.89), channel_id=1, source_target_pairs={{2,3},{3,2},{6,7},{7,6},{10,11},{11,10},{14,15},{15,14},{18,19},{1... | collective-permute-start | bytes 1966088 | tf_op jit(solution)/shard_map/ppermute | solution.py:197
where the time goes:
time: 109 us; the launch traced here: 108 us
  waiting for transfers between devices  59.2 us (54%)
  starting transfers between devices  23.3 us (21%)
  Pallas kernels  19.8 us (18%)
  local copies, waits for them, and re-layouts  2.67 us (2%)
  other arithmetic  2.37 us (2%)
    ppermute x12, waiting for transfers between devices, go(): return lax.ppermute(value, AXES, route[name])  59.2 us
    ppermute x12, starting transfers between devices, go(): return lax.ppermute(value, AXES, route[name])  23.3 us
    pallas_call x8, Pallas kernels, call(): pl.pallas_call(body, in_specs=[IN_SMEM] * scalars + [IN_VMEM] * (len(args...  19.8 us
    dynamic_slice x2, local copies, waits for them, and re-layouts, cut(): lax.dynamic_slice(v, (0, at), (rows, half))  2.64 us
    concatenate x2, other arithmetic, cut(): jnp.concatenate([lax.dynamic_slice(v, (0, at), (rows, half)) for v in (a,...  2.29 us
  transfers between devices with their start and end apart: 12, of which 9 were waited for; matrix products, arithmetic and copies ran while one was open for 2% of the time, Pallas kernels for 12%

commit v1 on v0

v1 whole, which is shorter than its diff:
```python
import functools

import jax
import jax.numpy as jnp
from jax import lax
from jax.experimental import pallas as pl
from jax.experimental.pallas import tpu as pltpu
from jax.sharding import PartitionSpec as P

BF = jnp.bfloat16
F32 = jnp.float32
AXES = ("blk", "rep")
LAST = (((1,), (1,)), ((), ()))
IN_VMEM = pl.BlockSpec(memory_space=pltpu.VMEM)
IN_SMEM = pl.BlockSpec(memory_space=pltpu.SMEM)
IN_PLACE = pl.BlockSpec(memory_space=pltpu.HBM)


def routes(n_blk):
    def at(b, r):
        return (b % n_blk) * 2 + r

    every = [(b, r) for b in range(n_blk) for r in (0, 1)]
    return {
        "swap": [(at(b, r), at(b, 1 - r)) for b, r in every],
        "back": [(at(b, r), at(b - 1, r)) for b, r in every],
        "back_flip": [(at(b, r), at(b - 1, r if b % 2 else 1 - r)) for b, r in every],
        "same_chip": [(at(b, r), at(b ^ 1, r)) for b, r in every],
        "fwd": [(at(b, r), at(b + 1, r)) for b, r in every],
        "fwd_flip": [(at(b, r), at(b + 1, 1 - r)) for b, r in every],
        "swap_even": [(at(b, r), at(b, 1 - r)) for b, r in every if b % 2 == 0],
    }


def call(body, args, outs, flops, scratch=(), scalars=0, raw=0):
    shapes = [jax.ShapeDtypeStruct(s, k) for s, k in outs]
    nbytes = sum(a.size * a.dtype.itemsize for a in (*args, *shapes))
    specs = [IN_SMEM] * scalars + [IN_PLACE] * raw + [IN_VMEM] * (len(args) - scalars - raw)
    return pl.pallas_call(
        body,
        in_specs=specs,
        out_specs=[IN_VMEM] * len(shapes),
        out_shape=shapes,
        scratch_shapes=list(scratch),
        compiler_params=pltpu.CompilerParams(vmem_limit_bytes=nbytes + (4 << 20)),
        cost_estimate=pl.CostEstimate(flops=flops, bytes_accessed=nbytes, transcendentals=0),
    )(*args)


def pre_body(picks, *refs):
    n = max(picks) + 1
    tokens, ws, (out, out16) = refs[:n], refs[n:-2], refs[-2:]
    for i, (w, k) in enumerate(zip(ws, picks)):
        s = lax.dot_general(w[...], tokens[k][...], LAST, preferred_element_type=F32)
        out[i] = s
        out16[i] = s.astype(BF)


def pre(tokens, picks, weights):
    hid, width = weights[0].shape
    rows = tokens[0].shape[0]
    shape = (len(weights), hid, rows)
    return call(
        functools.partial(pre_body, picks),
        (*tokens, *weights),
        [(shape, F32), (shape, BF)],
        2 * len(weights) * rows * width * hid,
    )


def pick_copies(odd, sources, buf, sems):
    rows = sources[0].shape[0]
    for i in range(2):
        dst = buf.at[pl.ds(i * rows, rows)]

        @pl.when(odd[0] == 1)
        def _():
            pltpu.make_async_copy(sources[i], dst, sems.at[i]).start()

        @pl.when(odd[0] == 0)
        def _():
            pltpu.make_async_copy(sources[2 + i], dst, sems.at[i]).start()


def pick_wait(sources, buf, sems, i):
    rows = sources[0].shape[0]
    pltpu.make_async_copy(sources[i], buf.at[pl.ds(i * rows, rows)], sems.at[i]).wait()


def pre2oth_body(odd, *refs):
    sources, (wg, wu, wd, out, out16, buf, sems) = refs[:4], refs[4:]
    rows = sources[0].shape[0]
    pick_copies(odd, sources, buf, sems)
    for i, (w, p) in enumerate(((wg, 0), (wu, 0), (wd, 1))):
        if i != 1:
            pick_wait(sources, buf, sems, p)
        t = buf[p * rows : (p + 1) * rows]
        s = lax.dot_general(w[...], t, LAST, preferred_element_type=F32)
        out[i] = s
        out16[i] = s.astype(BF)


def pre2oth(odd, sources, weights):
    rows, width = sources[0].shape
    hid = weights[0].shape[0]
    shape = (3, hid, rows)
    return call(
        pre2oth_body,
        (odd, *sources, *weights),
        [(shape, F32), (shape, BF)],
        6 * rows * width * hid,
        scratch=[pltpu.VMEM((2 * rows, width), BF), pltpu.SemaphoreType.DMA((2,))],
        scalars=1,
        raw=4,
    )


def act_body(pieces, chunks, joined, *refs):
    if joined:
        keep, extra, *refs = refs
    wg, wu, d, own, oth, turned = refs[-6:]
    at = 0
    for ps, rs in pieces:
        gate, up, ga = (refs[i][j] + refs[k][m].astype(F32) for (i, j), (k, m) in zip(ps, rs))
        sig = 1.0 / (1.0 + jnp.exp(-gate))
        silu = gate * sig
        dgate = ga * up * sig * (1.0 + gate * (1.0 - sig))
        dup = ga * silu
        n = gate.shape[1]
        part = pl.ds(at, n)
        d[0, :, part] = (silu * up).astype(BF)
        d[1, :, part] = dgate.astype(BF)
        d[2, :, part] = dup.astype(BF)
        turned[0, part, :] = dgate.T.astype(BF)
        turned[1, part, :] = dup.T.astype(BF)
        at += n
    rows, width = own.shape
    n = width // chunks

    @pl.loop(0, chunks)
    def _(c):
        cols = pl.ds(pl.multiple_of(c * n, n), n)
        s = jnp.dot(turned[0], wg[:, cols], preferred_element_type=F32)
        s += jnp.dot(turned[1], wu[:, cols], preferred_element_type=F32)
        own[:, cols] = s[:rows].astype(own.dtype)
        low = s[rows:]
        if joined:
            low += extra[:, cols].astype(F32) * keep[0].astype(F32)
        oth[:, cols] = low.astype(oth.dtype)


def act(arrays, pieces, wg, wu, rows, kinds, joined=()):
    hid, width = wg.shape
    return call(
        functools.partial(act_body, pieces, 5, len(joined)),
        (*joined, *arrays, wg, wu),
        [((3, hid, 2 * rows), BF)] + [((rows, width), t) for t in kinds],
        16 * rows * hid * width,
        scratch=[pltpu.VMEM((2, 2 * rows, hid), BF)],
        scalars=len(joined) // 2,
    )


def dw_body(chunks, odd, *refs):
    sources, (d1, d2, x0, g0, x1, g1, x2, g2, gg, gu, gd, buf, sems) = refs[:4], refs[4:]
    pick_copies(odd, sources, buf, sems)
    for i in range(2):
        pick_wait(sources, buf, sems, i)
    n = gg.shape[1] // chunks
    rows = x1.shape[0]
    top, low = pl.ds(0, rows), pl.ds(rows, rows)

    @pl.loop(0, chunks)
    def _(c):
        cols = pl.ds(pl.multiple_of(c * n, n), n)
        x = jnp.concatenate([x0[:, cols], x1[:, cols], x2[:, cols], buf[top, cols]], 0)
        g = jnp.concatenate([g0[:, cols], g1[:, cols], g2[:, cols], buf[low, cols]], 0)
        for i, out, t in ((1, gg, x), (2, gu, x), (0, gd, g)):
            d = jnp.concatenate([d1[i], d2[i]], 1)
            out[:, cols] = jnp.dot(d, t, preferred_element_type=F32).astype(BF)


def dw(odd, sources, d1, d2, tokens):
    hid = d1.shape[1]
    rows, width = sources[0].shape
    return call(
        functools.partial(dw_body, 5),
        (odd, *sources, d1, d2, *tokens),
        [((hid, width), BF)] * 3,
        24 * rows * hid * width,
        scratch=[pltpu.VMEM((2 * rows, width), BF), pltpu.SemaphoreType.DMA((2,))],
        scalars=1,
        raw=4,
    )


def last_body(where, own1, own2, left, flip, out):
    half = own1.shape[1]
    own = pl.ds(pl.multiple_of(where[1] * half, 128), half)
    oth = pl.ds(pl.multiple_of((1 - where[1]) * half, 128), half)
    out[:, own] = (own1[...] + own2[...].astype(F32)).astype(BF)

    @pl.when(where[0] == 1)
    def _():
        out[:, oth] = flip[...]

    @pl.when(where[0] == 0)
    def _():
        out[:, oth] = (left[...].astype(F32) + flip[...].astype(F32)).astype(BF)


def solution(mesh):
    route = routes(mesh.shape["blk"])

    def go(value, name):
        return lax.ppermute(value, AXES, route[name])

    def steps(inputs, upstream, w_gate_t, w_up_t, w_down):
        rows, width = inputs.shape
        half = width // 2
        weights = (w_gate_t, w_up_t, w_down)
        rep = lax.axis_index("rep").astype(jnp.int32)
        odd = (lax.axis_index("blk") % 2).astype(jnp.int32).reshape(1)
        cut = lambda a, at: lax.dynamic_slice(a, (0, at * half), (rows, half))
        x_snd, g_snd = cut(inputs, 1 - rep), cut(upstream, 1 - rep)
        x_own, g_own = (cut(a, rep) for a in lax.optimization_barrier((inputs, upstream)))
        x_oth, g_oth = go(x_snd, "swap"), go(g_snd, "swap")
        links = [go(x_snd, "back_flip"), go(g_snd, "back_flip")]
        p1_own, p1_own16 = pre([x_own, g_own], (0, 0, 1), weights)
        r1_oth = go(p1_own16, "swap")
        x2_own, g2_own = go(x_own, "back"), go(g_own, "back")
        p1_x, p1_x16 = pre([x_oth], (0, 0), weights[:2])
        p1_g, p1_g16 = pre([g_oth], (0,), weights[2:])
        r1_x, r1_g = go(p1_x16, "swap"), go(p1_g16, "swap")
        sources = (*links, go(x_oth, "same_chip"), go(g_oth, "same_chip"))
        three = lambda i: ((i, 0), (i, 1), (i, 2))
        split = lambda i: ((i, 0), (i, 1), (i + 1, 0))
        d1, own1, oth1 = act(
            (p1_own, r1_oth, p1_x, p1_g, r1_x, r1_g),
            ((three(0), split(4)), (split(2), three(1))),
            w_gate_t,
            w_up_t,
            rows,
            (F32, BF),
        )
        left = go(oth1, "swap_even")
        below = go(oth1, "same_chip")
        p2_oth, p2_oth16 = pre2oth(odd, sources, weights)
        r2_own = go(p2_oth16, "swap")
        p2_own, p2_own16 = pre([x2_own, g2_own], (0, 0, 1), weights)
        r2_oth = go(p2_own16, "swap")
        d2, own2, oth2 = act(
            (p2_own, p2_oth, r2_own, r2_oth),
            ((three(0), three(2)), (three(1), three(3))),
            w_gate_t,
            w_up_t,
            rows,
            (BF, BF),
            (1 - odd, below),
        )
        own2_home = go(own2, "fwd")
        flip = go(oth2, "fwd_flip")
        gg, gu, gd = dw(odd, sources, d1, d2, (x_own, g_own, x_oth, g_oth, x2_own, g2_own))
        (d_in,) = call(
            last_body,
            (jnp.stack([odd[0], rep]), own1, own2_home, left, flip),
            [((rows, width), BF)],
            2 * rows * width,
            scalars=1,
        )
        return d_in, gg, gu, gd

    tokens, weights = P(AXES, None), P("blk", "rep")
    return jax.shard_map(
        steps,
        mesh=mesh,
        in_specs=(tokens, tokens, weights, weights, weights),
        out_specs=(tokens, weights, weights, weights),
        check_vma=False,
    )
```

time: 109 us -> 112 us (1.028)
  the two profiles are of different devices: /device:TPU:1 before, /device:TPU:2 now
where the time goes in v1:
time: 112 us
  waiting for transfers between devices  42.1 us (38%)
  starting transfers between devices  34.4 us (31%)
  Pallas kernels  22.6 us (20%)
  local copies, waits for them, and re-layouts  11.6 us (10%)
    ppermute x17, waiting for transfers between devices, go(): return lax.ppermute(value, AXES, route[name])  42.1 us
    ppermute x17, starting transfers between devices, go(): return lax.ppermute(value, AXES, route[name])  34.4 us
    pallas_call x9, Pallas kernels, call(): pl.pallas_call(body, in_specs=specs, out_specs=[IN_VMEM] * len(shapes), o...  22.6 us
    unnamed x42, local copies, waits for them, and re-layouts  8.65 us
    dynamic_slice x4, local copies, waits for them, and re-layouts, steps(): cut = lambda a, at: lax.dynamic_slice(a, (0, at * half), (rows, half))  2.93 us
  transfers between devices with their start and end apart: 17, of which 5 were waited for; matrix products, arithmetic and copies ran while one was open for 2% of the time, Pallas kernels for 19%

profile of v1, /device:TPU:2, one launch (start us, length us, event | category | flops | bytes accessed | tf_op | source)
XLA Modules:
  0.0 111.6 jit_solution(4365882852790379508)
XLA Ops:
  0.6 0.0 copy-start
  0.6 0.0 copy-start.20
  0.7 1.3 %copy-done = bf16[128,5120]{1,0:T(8,128)(2,1)S(1)} copy-done((bf16[128,5120]{1,0:T(8,128)(2,1)S(1)}, bf16[128,5120]{1,0:T(8,128)(2,1)}, u32[]{:S(2)}) %copy-start) | copy-done | bytes 1310744
  2.0 0.9 constant_dynamic-slice_fusion.1
  2.8 2.2 %collective-permute-start.1 = (bf16[128,2560]{1,0:T(8,128)(2,1)}, bf16[128,2560]{1,0:T(8,128)(2,1)}, u32[]{:S(2)}, u32[]{:S(2)}) collective-permute-start(bf16[128,2560]{1,0:T(8,128)(2,1)} %constant_dynamic-slice_fusion.1), channel_id=1, source_target_pairs={{0,1},{1,0},{2,3},{3,2},{4,5},{5,4},{6,7},{7,6},{8,9},{9,8},{10,11... | collective-permute-start | bytes 1966088 | tf_op jit(solution)/shard_map/ppermute | solution.py:216
  5.1 0.9 constant_dynamic-slice_fusion
  6.0 0.0 collective-permute-start.2
  6.0 8.6 %collective-permute-start.6 = (bf16[128,2560]{1,0:T(8,128)(2,1)S(1)}, bf16[128,2560]{1,0:T(8,128)(2,1)S(1)}, u32[]{:S(2)}, u32[]{:S(2)}) collective-permute-start(bf16[128,2560]{1,0:T(8,128)(2,1)S(1)} %constant_dynamic-slice_fusion.3.refs_0_.refs_6_), channel_id=1, source_target_pairs={{0,254},{1,255},{2,0},{3,1},{4,2},{5,3},{6,4},{7,5},{8,6},{9,7},{1... | collective-permute-start | bytes 1966088 | tf_op jit(solution)/shard_map/ppermute | solution.py:216
  14.6 1.1 %constant_dynamic-slice_fusion.2.refs_1_.refs_7_ = bf16[128,2560]{1,0:T(8,128)(2,1)S(1)} fusion(bf16[128,5120]{1,0:T(8,128)(2,1)} %param.6, s32[]{:T(128)S(6)} %select_n.16), kind=kLoop, calls=%fused_computation.2 | loop fusion | bytes 1310724 | tf_op jit(solution)/shard_map/dynamic_slice | solution.py:224
  15.8 1.3 %collective-permute-start.7 = (bf16[128,2560]{1,0:T(8,128)(2,1)S(1)}, bf16[128,2560]{1,0:T(8,128)(2,1)S(1)}, u32[]{:S(2)}, u32[]{:S(2)}) collective-permute-start(bf16[128,2560]{1,0:T(8,128)(2,1)S(1)} %constant_dynamic-slice_fusion.2.refs_1_.refs_7_), channel_id=1, source_target_pairs={{0,254},{1,255},{2,0},{3,1},{4,2},{5,3},{6,4},{7,5},{8,6},{9,7},{1... | collective-permute-start | bytes 1966088 | tf_op jit(solution)/shard_map/ppermute | solution.py:216
  17.1 1.2 %copy-done.3 = bf16[216,2560]{1,0:T(8,128)(2,1)S(1)} copy-done((bf16[216,2560]{1,0:T(8,128)(2,1)S(1)}, bf16[216,2560]{1,0:T(8,128)(2,1)}, u32[]{:S(2)}) %copy-start.3) | copy-done | bytes 1105944
  18.3 1.0 shard_map.84
  19.4 1.5 %collective-permute-start = (bf16[3,216,128]{2,1,0:T(8,128)(2,1)S(1)}, bf16[3,216,128]{2,1,0:T(8,128)(2,1)S(1)}, u32[]{:S(2)}, u32[]{:S(2)}) collective-permute-start(bf16[3,216,128]{2,1,0:T(8,128)(2,1)S(1)} %get-tuple-element.28), channel_id=1, source_target_pairs={{0,1},{1,0},{2,3},{3,2},{4,5},{5,4},{6,7},{7,6},{8,9},{9,8},{10,11... | collective-permute-start | bytes 497672 | tf_op jit(solution)/shard_map/ppermute | solution.py:216
  20.9 14.1 %collective-permute-done.1.refs_0_.refs_8_ = bf16[128,2560]{1,0:T(8,128)(2,1)} collective-permute-done((bf16[128,2560]{1,0:T(8,128)(2,1)}, bf16[128,2560]{1,0:T(8,128)(2,1)}, u32[]{:S(2)}, u32[]{:S(2)}) %collective-permute-start.1) | collective-permute-done | bytes 655392 | tf_op jit(solution)/shard_map/ppermute | solution.py:216
  35.0 1.8 %shard_map.85 = (f32[2,216,128]{2,1,0:T(8,128)S(1)}, bf16[2,216,128]{2,1,0:T(8,128)(2,1)S(1)}) custom-call(bf16[128,2560]{1,0:T(8,128)(2,1)} %collective-permute-done.1.refs_0_.refs_8_, bf16[216,2560]{1,0:T(8,128)(2,1)S(1)} %copy-done.2, bf16[216,2560]{1,0:T(8,128)(2,1)S(1)} %copy-done.3), custom_call_target="tpu_custom_call" | custom-call | flops 283115520 | bytes 3198976 | tf_op jit(solution)/shard_map/pallas_call | solution.py:39
  36.9 2.1 %collective-permute-start.3 = (bf16[2,216,128]{2,1,0:T(8,128)(2,1)S(1)}, bf16[2,216,128]{2,1,0:T(8,128)(2,1)S(1)}, u32[]{:S(2)}, u32[]{:S(2)}) collective-permute-start(bf16[2,216,128]{2,1,0:T(8,128)(2,1)S(1)} %get-tuple-element.31), channel_id=1, source_target_pairs={{0,1},{1,0},{2,3},{3,2},{4,5},{5,4},{6,7},{7,6},{8,9},{9,8},{10,11... | collective-permute-start | bytes 331784 | tf_op jit(solution)/shard_map/ppermute | solution.py:216
  39.0 10.1 %collective-permute-done.2.refs_0_.refs_9_ = bf16[128,2560]{1,0:T(8,128)(2,1)} collective-permute-done((bf16[128,2560]{1,0:T(8,128)(2,1)}, bf16[128,2560]{1,0:T(8,128)(2,1)}, u32[]{:S(2)}, u32[]{:S(2)}) %collective-permute-start.2) | collective-permute-done | bytes 655392 | tf_op jit(solution)/shard_map/ppermute | solution.py:216
  49.1 1.5 %shard_map.86 = (f32[1,216,128]{2,1,0:T(8,128)S(1)}, bf16[1,216,128]{2,1,0:T(8,128)(2,1)S(1)}) custom-call(bf16[128,2560]{1,0:T(8,128)(2,1)} %collective-permute-done.2.refs_0_.refs_9_, bf16[216,2560]{1,0:T(8,128)(2,1)S(1)} %copy-done.1), custom_call_target="tpu_custom_call" | custom-call | flops 141557760 | bytes 1927168 | tf_op jit(solution)/shard_map/pallas_call | solution.py:39
  50.6 2.0 %collective-permute-start.4 = (bf16[1,216,128]{2,1,0:T(8,128)(2,1)S(1)}, bf16[1,216,128]{2,1,0:T(8,128)(2,1)S(1)}, u32[]{:S(2)}, u32[]{:S(2)}) collective-permute-start(bf16[1,216,128]{2,1,0:T(8,128)(2,1)S(1)} %get-tuple-element.32), channel_id=1, source_target_pairs={{0,1},{1,0},{2,3},{3,2},{4,5},{5,4},{6,7},{7,6},{8,9},{9,8},{10,11... | collective-permute-start | bytes 165896 | tf_op jit(solution)/shard_map/ppermute | solution.py:216
  52.6 0.0 copy-start.10
  52.6 9.7 %collective-permute-start.9 = (bf16[128,2560]{1,0:T(8,128)(2,1)}, bf16[128,2560]{1,0:T(8,128)(2,1)}, u32[]{:S(2)}, u32[]{:S(2)}) collective-permute-start(bf16[128,2560]{1,0:T(8,128)(2,1)} %constant_dynamic-slice_fusion), channel_id=1, source_target_pairs={{0,255},{1,254},{2,0},{3,1},{4,3},{5,2},{6,4},{7,5},{8,7},{9,6},{1... | collective-permute-start | bytes 1966088 | tf_op jit(solution)/shard_map/ppermute | solution.py:216
  62.3 0.0 collective-permute-done.4.refs_5_
  62.3 0.0 collective-permute-start.10
  62.3 0.5 collective-permute-start.11
  62.8 2.6 %shard_map.87 = (bf16[3,216,256]{2,1,0:T(8,128)(2,1)S(1)}, f32[128,2560]{1,0:T(8,128)S(1)}, bf16[128,2560]{1,0:T(8,128)(2,1)}) custom-call(f32[3,216,128]{2,1,0:T(8,128)S(1)} %get-tuple-element.27.refs_0_, bf16[3,216,128]{2,1,0:T(8,128)(2,1)S(1)} %collective-permute-done.refs_1_, f32[2,216,128]{2,1,0:T(8,128)S(1)} %get-tuple-element.29.refs_2_, ...), custom_call_target="tpu_custom_call" | custom-call | flops 1132462080 | bytes 5505024 | tf_op jit(solution)/shard_map/pallas_call | solution.py:39
  65.4 1.1 copy-done.16
  66.4 0.7 copy-done.18
  67.2 0.9 copy-done.13
  68.0 0.1 collective-permute-start.5
  68.1 1.2 %copy-done.4 = bf16[216,2560]{1,0:T(8,128)(2,1)S(1)} copy-done((bf16[216,2560]{1,0:T(8,128)(2,1)S(1)}, bf16[216,2560]{1,0:T(8,128)(2,1)}, u32[]{:S(2)}) %copy-start.4) | copy-done | bytes 1105944
  69.4 1.1 copy-done.11
  70.4 1.1 copy-done.14
  71.5 1.0 shard_map.88
  72.6 0.0 collective-permute-done.8.refs_0_
  72.6 1.9 %collective-permute-start.13 = (bf16[3,216,128]{2,1,0:T(8,128)(2,1)S(1)}, bf16[3,216,128]{2,1,0:T(8,128)(2,1)S(1)}, u32[]{:S(2)}, u32[]{:S(2)}) collective-permute-start(bf16[3,216,128]{2,1,0:T(8,128)(2,1)S(1)} %get-tuple-element.38), channel_id=1, source_target_pairs={{0,1},{1,0},{2,3},{3,2},{4,5},{5,4},{6,7},{7,6},{8,9},{9,8},{10,11... | collective-permute-start | bytes 497672 | tf_op jit(solution)/shard_map/ppermute | solution.py:216
  74.5 2.9 %shard_map.89 = (f32[3,216,128]{2,1,0:T(8,128)S(1)}, bf16[3,216,128]{2,1,0:T(8,128)(2,1)S(1)}) custom-call(s32[1]{0:T(128)} %bitcast.odd, bf16[128,2560]{1,0:T(8,128)(2,1)} %collective-permute-done.8.refs_0_, bf16[128,2560]{1,0:T(8,128)(2,1)} %collective-permute-done.9.refs_1_, bf16[128,2560]{1,0:T(8,128)(2,1)} %collective-permute-done.10.refs_2_, ...), custom_call_target="tpu_custom_call" | custom-call | flops 424673280 | bytes 6436868 | tf_op jit(solution)/shard_map/pallas_call | solution.py:39
  77.4 0.3 collective-permute-start.12
  77.7 3.9 %collective-permute-start.15 = (bf16[128,2560]{1,0:T(8,128)(2,1)}, bf16[128,2560]{1,0:T(8,128)(2,1)S(1)}, u32[]{:S(2)}, u32[]{:S(2)}) collective-permute-start(bf16[128,2560]{1,0:T(8,128)(2,1)} %get-tuple-element.34), channel_id=1, source_target_pairs={{0,1},{1,0},{4,5},{5,4},{8,9},{9,8},{12,13},{13,12},{16,17},{17,16... | collective-permute-start | bytes 1966088 | tf_op jit(solution)/shard_map/ppermute | solution.py:216
  81.6 2.1 %collective-permute-done.12.refs_4_ = bf16[3,216,128]{2,1,0:T(8,128)(2,1)S(1)} collective-permute-done((bf16[3,216,128]{2,1,0:T(8,128)(2,1)S(1)}, bf16[3,216,128]{2,1,0:T(8,128)(2,1)S(1)}, u32[]{:S(2)}, u32[]{:S(2)}) %collective-permute-start.12) | collective-permute-done | bytes 165920 | tf_op jit(solution)/shard_map/ppermute | solution.py:216
  83.8 3.0 %shard_map.90 = (bf16[3,216,256]{2,1,0:T(8,128)(2,1)S(1)}, bf16[128,2560]{1,0:T(8,128)(2,1)S(1)}, bf16[128,2560]{1,0:T(8,128)(2,1)S(1)}) custom-call(s32[1]{0:T(128)S(6)} %sub.8.refs_0_, bf16[128,2560]{1,0:T(8,128)(2,1)} %collective-permute-done.5.refs_1_, f32[3,216,128]{2,1,0:T(8,128)S(1)} %get-tuple-element.35.refs_2_, ...), custom_call_target="tpu_custom_call" | custom-call | flops 1132462080 | bytes 5505028 | tf_op jit(solution)/shard_map/pallas_call | solution.py:39
  86.8 0.1 collective-permute-start.14
  86.9 0.1 collective-permute-start.16
  87.0 0.1 pad_add_fusion.where
  87.1 0.0 copy-start.17
  87.1 6.8 %shard_map.92 = (bf16[216,2560]{1,0:T(8,128)(2,1)}, bf16[216,2560]{1,0:T(8,128)(2,1)}, bf16[216,2560]{1,0:T(8,128)(2,1)}) custom-call(s32[1]{0:T(128)} %bitcast.odd, bf16[128,2560]{1,0:T(8,128)(2,1)} %collective-permute-done.8.refs_0_, bf16[128,2560]{1,0:T(8,128)(2,1)} %collective-permute-done.9.refs_1_, bf16[128,2560]{1,0:T(8,128)(2,1)} %collective-permute-done.10.refs_2_, ...), custom_call_target="tpu_custom_call" | custom-call | flops 1698693120 | bytes 10534916 | tf_op jit(solution)/shard_map/pallas_call | solution.py:39
  93.9 10.1 %collective-permute-done.14.own2 = bf16[128,2560]{1,0:T(8,128)(2,1)S(1)} collective-permute-done((bf16[128,2560]{1,0:T(8,128)(2,1)S(1)}, bf16[128,2560]{1,0:T(8,128)(2,1)S(1)}, u32[]{:S(2)}, u32[]{:S(2)}) %collective-permute-start.14) | collective-permute-done | bytes 655392 | tf_op jit(solution)/shard_map/ppermute | solution.py:216
  104.1 5.6 %collective-permute-done.16.flip = bf16[128,2560]{1,0:T(8,128)(2,1)S(1)} collective-permute-done((bf16[128,2560]{1,0:T(8,128)(2,1)S(1)}, bf16[128,2560]{1,0:T(8,128)(2,1)S(1)}, u32[]{:S(2)}, u32[]{:S(2)}) %collective-permute-start.16) | collective-permute-done | bytes 655392 | tf_op jit(solution)/shard_map/ppermute | solution.py:216
  109.7 1.9 %shard_map.91 = bf16[128,5120]{1,0:T(8,128)(2,1)} custom-call(s32[2]{0:T(128)S(1)} %pad_add_fusion.where, f32[128,2560]{1,0:T(8,128)S(1)} %copy-done.17, bf16[128,2560]{1,0:T(8,128)(2,1)S(1)} %collective-permute-done.14.own2, bf16[128,2560]{1,0:T(8,128)(2,1)S(1)} %collective-permute-done.15.left, bf16[128,2560]{1,0:T(8,128)(2,1)S(1)} %collective-permute-done.16.flip), custom_call_target="tpu_custom_call" | custom-call | flops 1310720 | bytes 4587528 | tf_op jit(solution)/shard_map/pallas_call | solution.py:39
  (42 shorter events, 0.1 us)
Async XLA Ops:
  0.6 1.3 %copy-start = (bf16[128,5120]{1,0:T(8,128)(2,1)S(1)}, bf16[128,5120]{1,0:T(8,128)(2,1)}, u32[]{:S(2)}) copy-start(bf16[128,5120]{1,0:T(8,128)(2,1)} %param.5) | copy-start | bytes 3932164
  0.6 4.4 %copy-start.20 = (bf16[128,5120]{1,0:T(8,128)(2,1)S(1)}, bf16[128,5120]{1,0:T(8,128)(2,1)}, u32[]{:S(2)}) copy-start(bf16[128,5120]{1,0:T(8,128)(2,1)} %param.6) | copy-start | bytes 3932164
  2.8 32.2 %collective-permute-start.1 = (bf16[128,2560]{1,0:T(8,128)(2,1)}, bf16[128,2560]{1,0:T(8,128)(2,1)}, u32[]{:S(2)}, u32[]{:S(2)}) collective-permute-start(bf16[128,2560]{1,0:T(8,128)(2,1)} %constant_dynamic-slice_fusion.1), channel_id=1, source_target_pairs={{0,1},{1,0},{2,3},{3,2},{4,5},{5,4},{6,7},{7,6},{8,9},{9,8},{10,11... | collective-permute-start | bytes 1966088 | tf_op jit(solution)/shard_map/ppermute | solution.py:216
  6.0 43.1 %collective-permute-start.2 = (bf16[128,2560]{1,0:T(8,128)(2,1)}, bf16[128,2560]{1,0:T(8,128)(2,1)}, u32[]{:S(2)}, u32[]{:S(2)}) collective-permute-start(bf16[128,2560]{1,0:T(8,128)(2,1)} %constant_dynamic-slice_fusion), channel_id=1, source_target_pairs={{0,1},{1,0},{2,3},{3,2},{4,5},{5,4},{6,7},{7,6},{8,9},{9,8},{10,11... | collective-permute-start | bytes 1966088 | tf_op jit(solution)/shard_map/ppermute | solution.py:216
  6.0 11.1 %copy-start.1 = (bf16[216,2560]{1,0:T(8,128)(2,1)S(1)}, bf16[216,2560]{1,0:T(8,128)(2,1)}, u32[]{:S(2)}) copy-start(bf16[216,2560]{1,0:T(8,128)(2,1)} %refs_6_.4) | copy-start | bytes 3317764
  6.0 11.1 %copy-start.2 = (bf16[216,2560]{1,0:T(8,128)(2,1)S(1)}, bf16[216,2560]{1,0:T(8,128)(2,1)}, u32[]{:S(2)}) copy-start(bf16[216,2560]{1,0:T(8,128)(2,1)} %refs_6_.5) | copy-start | bytes 3317764
  6.0 13.4 %copy-start.6 = (bf16[128,2560]{1,0:T(8,128)(2,1)}, bf16[128,2560]{1,0:T(8,128)(2,1)S(1)}, u32[]{:S(2)}) copy-start(bf16[128,2560]{1,0:T(8,128)(2,1)S(1)} %constant_dynamic-slice_fusion.3.refs_0_.refs_6_) | copy-start | bytes 1966084
  6.0 46.6 %collective-permute-start.6 = (bf16[128,2560]{1,0:T(8,128)(2,1)S(1)}, bf16[128,2560]{1,0:T(8,128)(2,1)S(1)}, u32[]{:S(2)}, u32[]{:S(2)}) collective-permute-start(bf16[128,2560]{1,0:T(8,128)(2,1)S(1)} %constant_dynamic-slice_fusion.3.refs_0_.refs_6_), channel_id=1, source_target_pairs={{0,254},{1,255},{2,0},{3,1},{4,2},{5,3},{6,4},{7,5},{8,6},{9,7},{1... | collective-permute-start | bytes 1966088 | tf_op jit(solution)/shard_map/ppermute | solution.py:216
  15.8 3.6 %copy-start.8 = (bf16[128,2560]{1,0:T(8,128)(2,1)}, bf16[128,2560]{1,0:T(8,128)(2,1)S(1)}, u32[]{:S(2)}) copy-start(bf16[128,2560]{1,0:T(8,128)(2,1)S(1)} %constant_dynamic-slice_fusion.2.refs_1_.refs_7_) | copy-start | bytes 1966084
  15.8 51.4 %collective-permute-start.7 = (bf16[128,2560]{1,0:T(8,128)(2,1)S(1)}, bf16[128,2560]{1,0:T(8,128)(2,1)S(1)}, u32[]{:S(2)}, u32[]{:S(2)}) collective-permute-start(bf16[128,2560]{1,0:T(8,128)(2,1)S(1)} %constant_dynamic-slice_fusion.2.refs_1_.refs_7_), channel_id=1, source_target_pairs={{0,254},{1,255},{2,0},{3,1},{4,2},{5,3},{6,4},{7,5},{8,6},{9,7},{1... | collective-permute-start | bytes 1966088 | tf_op jit(solution)/shard_map/ppermute | solution.py:216
  17.1 1.2 %copy-start.3 = (bf16[216,2560]{1,0:T(8,128)(2,1)S(1)}, bf16[216,2560]{1,0:T(8,128)(2,1)}, u32[]{:S(2)}) copy-start(bf16[216,2560]{1,0:T(8,128)(2,1)} %refs_7_.3) | copy-start | bytes 3317764
  19.4 33.2 %collective-permute-start = (bf16[3,216,128]{2,1,0:T(8,128)(2,1)S(1)}, bf16[3,216,128]{2,1,0:T(8,128)(2,1)S(1)}, u32[]{:S(2)}, u32[]{:S(2)}) collective-permute-start(bf16[3,216,128]{2,1,0:T(8,128)(2,1)S(1)} %get-tuple-element.28), channel_id=1, source_target_pairs={{0,1},{1,0},{2,3},{3,2},{4,5},{5,4},{6,7},{7,6},{8,9},{9,8},{10,11... | collective-permute-start | bytes 497672 | tf_op jit(solution)/shard_map/ppermute | solution.py:216
  36.9 25.4 %collective-permute-start.3 = (bf16[2,216,128]{2,1,0:T(8,128)(2,1)S(1)}, bf16[2,216,128]{2,1,0:T(8,128)(2,1)S(1)}, u32[]{:S(2)}, u32[]{:S(2)}) collective-permute-start(bf16[2,216,128]{2,1,0:T(8,128)(2,1)S(1)} %get-tuple-element.31), channel_id=1, source_target_pairs={{0,1},{1,0},{2,3},{3,2},{4,5},{5,4},{6,7},{7,6},{8,9},{9,8},{10,11... | collective-permute-start | bytes 331784 | tf_op jit(solution)/shard_map/ppermute | solution.py:216
  50.6 11.7 %collective-permute-start.4 = (bf16[1,216,128]{2,1,0:T(8,128)(2,1)S(1)}, bf16[1,216,128]{2,1,0:T(8,128)(2,1)S(1)}, u32[]{:S(2)}, u32[]{:S(2)}) collective-permute-start(bf16[1,216,128]{2,1,0:T(8,128)(2,1)S(1)} %get-tuple-element.32), channel_id=1, source_target_pairs={{0,1},{1,0},{2,3},{3,2},{4,5},{5,4},{6,7},{7,6},{8,9},{9,8},{10,11... | collective-permute-start | bytes 165896 | tf_op jit(solution)/shard_map/ppermute | solution.py:216
  52.6 20.0 %collective-permute-start.8 = (bf16[128,2560]{1,0:T(8,128)(2,1)}, bf16[128,2560]{1,0:T(8,128)(2,1)}, u32[]{:S(2)}, u32[]{:S(2)}) collective-permute-start(bf16[128,2560]{1,0:T(8,128)(2,1)} %constant_dynamic-slice_fusion.1), channel_id=1, source_target_pairs={{0,255},{1,254},{2,0},{3,1},{4,3},{5,2},{6,4},{7,5},{8,7},{9,6},{1... | collective-permute-start | bytes 1966088 | tf_op jit(solution)/shard_map/ppermute | solution.py:216
  52.6 12.8 %copy-start.10 = (bf16[128,2560]{1,0:T(8,128)(2,1)}, bf16[128,2560]{1,0:T(8,128)(2,1)S(1)}, u32[]{:S(2)}) copy-start(bf16[128,2560]{1,0:T(8,128)(2,1)S(1)} %collective-permute-done.6.refs_0_.refs_10_) | copy-start | bytes 1966084
  52.6 21.9 %collective-permute-start.9 = (bf16[128,2560]{1,0:T(8,128)(2,1)}, bf16[128,2560]{1,0:T(8,128)(2,1)}, u32[]{:S(2)}, u32[]{:S(2)}) collective-permute-start(bf16[128,2560]{1,0:T(8,128)(2,1)} %constant_dynamic-slice_fusion), channel_id=1, source_target_pairs={{0,255},{1,254},{2,0},{3,1},{4,3},{5,2},{6,4},{7,5},{8,7},{9,6},{1... | collective-permute-start | bytes 1966088 | tf_op jit(solution)/shard_map/ppermute | solution.py:216
  62.3 12.2 %collective-permute-start.10 = (bf16[128,2560]{1,0:T(8,128)(2,1)}, bf16[128,2560]{1,0:T(8,128)(2,1)}, u32[]{:S(2)}, u32[]{:S(2)}) collective-permute-start(bf16[128,2560]{1,0:T(8,128)(2,1)} %collective-permute-done.1.refs_0_.refs_8_), channel_id=1, source_target_pairs={{0,2},{1,3},{2,0},{3,1},{4,6},{5,7},{6,4},{7,5},{8,10},{9,11},{10,... | collective-permute-start | bytes 1966088 | tf_op jit(solution)/shard_map/ppermute | solution.py:216
  62.3 12.2 %collective-permute-start.11 = (bf16[128,2560]{1,0:T(8,128)(2,1)}, bf16[128,2560]{1,0:T(8,128)(2,1)}, u32[]{:S(2)}, u32[]{:S(2)}) collective-permute-start(bf16[128,2560]{1,0:T(8,128)(2,1)} %collective-permute-done.2.refs_0_.refs_9_), channel_id=1, source_target_pairs={{0,2},{1,3},{2,0},{3,1},{4,6},{5,7},{6,4},{7,5},{8,10},{9,11},{10,... | collective-permute-start | bytes 1966088 | tf_op jit(solution)/shard_map/ppermute | solution.py:216
  65.4 1.1 copy-start.16
  66.4 0.7 copy-start.18
  67.2 0.9 copy-start.13
  68.0 13.6 %collective-permute-start.5 = (bf16[128,2560]{1,0:T(8,128)(2,1)}, bf16[128,2560]{1,0:T(8,128)(2,1)}, u32[]{:S(2)}, u32[]{:S(2)}) collective-permute-start(bf16[128,2560]{1,0:T(8,128)(2,1)} %get-tuple-element.34), channel_id=1, source_target_pairs={{0,2},{1,3},{2,0},{3,1},{4,6},{5,7},{6,4},{7,5},{8,10},{9,11},{10,... | collective-permute-start | bytes 1966088 | tf_op jit(solution)/shard_map/ppermute | solution.py:216
  68.1 1.2 %copy-start.4 = (bf16[216,2560]{1,0:T(8,128)(2,1)S(1)}, bf16[216,2560]{1,0:T(8,128)(2,1)}, u32[]{:S(2)}) copy-start(bf16[216,2560]{1,0:T(8,128)(2,1)} %refs_7_.3) | copy-start | bytes 3317764
  69.4 1.1 copy-start.11
  70.4 1.1 copy-start.14
  71.5 3.0 %copy-start.5 = (bf16[216,2560]{1,0:T(8,128)(2,1)S(1)}, bf16[216,2560]{1,0:T(8,128)(2,1)}, u32[]{:S(2)}) copy-start(bf16[216,2560]{1,0:T(8,128)(2,1)} %refs_7_.3) | copy-start | bytes 3317764
  72.6 9.0 %collective-permute-start.13 = (bf16[3,216,128]{2,1,0:T(8,128)(2,1)S(1)}, bf16[3,216,128]{2,1,0:T(8,128)(2,1)S(1)}, u32[]{:S(2)}, u32[]{:S(2)}) collective-permute-start(bf16[3,216,128]{2,1,0:T(8,128)(2,1)S(1)} %get-tuple-element.38), channel_id=1, source_target_pairs={{0,1},{1,0},{2,3},{3,2},{4,5},{5,4},{6,7},{7,6},{8,9},{9,8},{10,11... | collective-permute-start | bytes 497672 | tf_op jit(solution)/shard_map/ppermute | solution.py:216
  77.4 6.4 %collective-permute-start.12 = (bf16[3,216,128]{2,1,0:T(8,128)(2,1)S(1)}, bf16[3,216,128]{2,1,0:T(8,128)(2,1)S(1)}, u32[]{:S(2)}, u32[]{:S(2)}) collective-permute-start(bf16[3,216,128]{2,1,0:T(8,128)(2,1)S(1)} %get-tuple-element.37), channel_id=1, source_target_pairs={{0,1},{1,0},{2,3},{3,2},{4,5},{5,4},{6,7},{7,6},{8,9},{9,8},{10,11... | collective-permute-start | bytes 497672 | tf_op jit(solution)/shard_map/ppermute | solution.py:216
  77.7 16.2 %collective-permute-start.15 = (bf16[128,2560]{1,0:T(8,128)(2,1)}, bf16[128,2560]{1,0:T(8,128)(2,1)S(1)}, u32[]{:S(2)}, u32[]{:S(2)}) collective-permute-start(bf16[128,2560]{1,0:T(8,128)(2,1)} %get-tuple-element.34), channel_id=1, source_target_pairs={{0,1},{1,0},{4,5},{5,4},{8,9},{9,8},{12,13},{13,12},{16,17},{17,16... | collective-permute-start | bytes 1966088 | tf_op jit(solution)/shard_map/ppermute | solution.py:216
  83.8 3.3 %copy-start.7 = (bf16[128,2560]{1,0:T(8,128)(2,1)S(1)}, bf16[128,2560]{1,0:T(8,128)(2,1)}, u32[]{:S(2)}) copy-start(bf16[128,2560]{1,0:T(8,128)(2,1)} %copy-done.6) | copy-start | bytes 1966084
  83.8 3.3 %copy-start.9 = (bf16[128,2560]{1,0:T(8,128)(2,1)S(1)}, bf16[128,2560]{1,0:T(8,128)(2,1)}, u32[]{:S(2)}) copy-start(bf16[128,2560]{1,0:T(8,128)(2,1)} %copy-done.8) | copy-start | bytes 1966084
  83.8 3.3 %copy-start.12 = (bf16[128,2560]{1,0:T(8,128)(2,1)S(1)}, bf16[128,2560]{1,0:T(8,128)(2,1)}, u32[]{:S(2)}) copy-start(bf16[128,2560]{1,0:T(8,128)(2,1)} %copy-done.10) | copy-start | bytes 1966084
  83.8 3.3 %copy-start.15 = (bf16[128,2560]{1,0:T(8,128)(2,1)S(1)}, bf16[128,2560]{1,0:T(8,128)(2,1)}, u32[]{:S(2)}) copy-start(bf16[128,2560]{1,0:T(8,128)(2,1)} %copy-done.13) | copy-start | bytes 1966084
  83.8 3.3 %copy-start.19 = (bf16[3,216,256]{2,1,0:T(8,128)(2,1)S(1)}, bf16[3,216,256]{2,1,0:T(8,128)(2,1)}, u32[]{:S(2)}) copy-start(bf16[3,216,256]{2,1,0:T(8,128)(2,1)} %copy-done.18) | copy-start | bytes 995332
  86.8 17.3 %collective-permute-start.14 = (bf16[128,2560]{1,0:T(8,128)(2,1)S(1)}, bf16[128,2560]{1,0:T(8,128)(2,1)S(1)}, u32[]{:S(2)}, u32[]{:S(2)}) collective-permute-start(bf16[128,2560]{1,0:T(8,128)(2,1)S(1)} %get-tuple-element.39), channel_id=1, source_target_pairs={{0,2},{1,3},{2,4},{3,5},{4,6},{5,7},{6,8},{7,9},{8,10},{9,11},{10,... | collective-permute-start | bytes 1966088 | tf_op jit(solution)/shard_map/ppermute | solution.py:216
  86.9 22.8 %collective-permute-start.16 = (bf16[128,2560]{1,0:T(8,128)(2,1)S(1)}, bf16[128,2560]{1,0:T(8,128)(2,1)S(1)}, u32[]{:S(2)}, u32[]{:S(2)}) collective-permute-start(bf16[128,2560]{1,0:T(8,128)(2,1)S(1)} %get-tuple-element.40), channel_id=1, source_target_pairs={{0,3},{1,2},{2,5},{3,4},{4,7},{5,6},{6,9},{7,8},{8,11},{9,10},{10,... | collective-permute-start | bytes 1966088 | tf_op jit(solution)/shard_map/ppermute | solution.py:216
  87.1 22.6 %copy-start.17 = (f32[128,2560]{1,0:T(8,128)S(1)}, f32[128,2560]{1,0:T(8,128)}, u32[]{:S(2)}) copy-start(f32[128,2560]{1,0:T(8,128)} %copy-done.16) | copy-start | bytes 3932164

commit v2 on v1

--- a/solution.py
+++ b/solution.py
@@ -194,19 +194,41 @@
     )
 
 
-def last_body(where, own1, own2, left, flip, out):
-    half = own1.shape[1]
-    own = pl.ds(pl.multiple_of(where[1] * half, 128), half)
-    oth = pl.ds(pl.multiple_of((1 - where[1]) * half, 128), half)
-    out[:, own] = (own1[...] + own2[...].astype(F32)).astype(BF)
-
+def put(at, buf, out, sem):
+    half = buf.shape[1]
+    cols = pl.ds(pl.multiple_of(at * half, 128), half)
+    copy = pltpu.make_async_copy(buf, out.at[:, cols], sem)
+    copy.start()
+    copy.wait()
+
+
+def own_body(where, a, b, out, buf, sem):
+    buf[...] = (a[...] + b[...].astype(F32)).astype(BF)
+    put(where[1], buf, out, sem)
+
+
+def oth_body(where, _, left, flip, out, buf, sem):
     @pl.when(where[0] == 1)
     def _():
-        out[:, oth] = flip[...]
+        buf[...] = flip[...]
 
     @pl.when(where[0] == 0)
     def _():
-        out[:, oth] = (left[...].astype(F32) + flip[...].astype(F32)).astype(BF)
+        buf[...] = (left[...].astype(F32) + flip[...].astype(F32)).astype(BF)
+
+    put(1 - where[1], buf, out, sem)
+
+
+def half_out(body, where, args, shape, base=()):
+    return pl.pallas_call(
+        body,
+        in_specs=[IN_SMEM] + [IN_PLACE] * len(base) + [IN_VMEM] * len(args),
+        out_specs=IN_PLACE,
+        out_shape=jax.ShapeDtypeStruct(shape, BF),
+        scratch_shapes=[pltpu.VMEM(args[0].shape, BF), pltpu.SemaphoreType.DMA],
+        input_output_aliases={1: 0} if base else {},
+        compiler_params=pltpu.CompilerParams(vmem_limit_bytes=8 << 20),
+    )(where, *base, *args)
 
 
 def solution(mesh):
@@ -261,13 +283,9 @@
         own2_home = go(own2, "fwd")
         flip = go(oth2, "fwd_flip")
         gg, gu, gd = dw(odd, sources, d1, d2, (x_own, g_own, x_oth, g_oth, x2_own, g2_own))
-        (d_in,) = call(
-            last_body,
-            (jnp.stack([odd[0], rep]), own1, own2_home, left, flip),
-            [((rows, width), BF)],
-            2 * rows * width,
-            scalars=1,
-        )
+        where = jnp.stack([odd[0], rep])
+        d_in = half_out(own_body, where, (own1, own2_home), (rows, width))
+        d_in = half_out(oth_body, where, (left, flip), (rows, width), (d_in,))
         return d_in, gg, gu, gd
 
     tokens, weights = P(AXES, None), P("blk", "rep")

time: 112 us -> 113 us (level)
  the two profiles are of different devices: /device:TPU:2 before, /device:TPU:1 now
where the time goes in v2:
time: 113 us; the launch traced here: 112 us
  waiting for transfers between devices  39.9 us (35%)
  starting transfers between devices  36 us (32%)
  Pallas kernels  23.6 us (21%)
  local copies, waits for them, and re-layouts  11.6 us (10%)
    ppermute x17, waiting for transfers between devices, go(): return lax.ppermute(value, AXES, route[name])  39.9 us
    ppermute x17, starting transfers between devices, go(): return lax.ppermute(value, AXES, route[name])  36 us
    pallas_call x8, Pallas kernels, call(): pl.pallas_call(body, in_specs=specs, out_specs=[IN_VMEM] * len(shapes), o...  20.7 us
    unnamed x42, local copies, waits for them, and re-layouts  8.7 us
    pallas_call x2, Pallas kernels, half_out(): pl.pallas_call(body, in_specs=[IN_SMEM] + [IN_PLACE] * len(base) + [IN_VM...  2.96 us
    dynamic_slice x4, local copies, waits for them, and re-layouts, steps(): cut = lambda a, at: lax.dynamic_slice(a, (0, at * half), (rows, half))  2.93 us
  transfers between devices with their start and end apart: 17, of which 6 were waited for; matrix products, arithmetic and copies ran while one was open for 2% of the time, Pallas kernels for 17%

profile of v2, /device:TPU:1, one launch (start us, length us, event | category | flops | bytes accessed | tf_op | source)
XLA Modules:
  0.0 112.1 jit_solution(6189620489207988169)
XLA Ops:
  0.6 0.0 copy-start
  0.6 0.0 copy-start.20
  0.7 1.3 %copy-done = bf16[128,5120]{1,0:T(8,128)(2,1)S(1)} copy-done((bf16[128,5120]{1,0:T(8,128)(2,1)S(1)}, bf16[128,5120]{1,0:T(8,128)(2,1)}, u32[]{:S(2)}) %copy-start) | copy-done | bytes 1310744
  2.0 0.9 constant_dynamic-slice_fusion.1
  2.8 2.0 %collective-permute-start.1 = (bf16[128,2560]{1,0:T(8,128)(2,1)}, bf16[128,2560]{1,0:T(8,128)(2,1)}, u32[]{:S(2)}, u32[]{:S(2)}) collective-permute-start(bf16[128,2560]{1,0:T(8,128)(2,1)} %constant_dynamic-slice_fusion.1), channel_id=1, source_target_pairs={{0,1},{1,0},{2,3},{3,2},{4,5},{5,4},{6,7},{7,6},{8,9},{9,8},{10,11... | collective-permute-start | bytes 1966088 | tf_op jit(solution)/shard_map/ppermute | solution.py:238
  4.9 0.9 constant_dynamic-slice_fusion
  5.8 3.3 %collective-permute-start.6 = (bf16[128,2560]{1,0:T(8,128)(2,1)S(1)}, bf16[128,2560]{1,0:T(8,128)(2,1)S(1)}, u32[]{:S(2)}, u32[]{:S(2)}) collective-permute-start(bf16[128,2560]{1,0:T(8,128)(2,1)S(1)} %constant_dynamic-slice_fusion.3.refs_0_.refs_6_), channel_id=1, source_target_pairs={{0,254},{1,255},{2,0},{3,1},{4,2},{5,3},{6,4},{7,5},{8,6},{9,7},{1... | collective-permute-start | bytes 1966088 | tf_op jit(solution)/shard_map/ppermute | solution.py:238
  9.1 1.1 %constant_dynamic-slice_fusion.2.refs_1_.refs_7_ = bf16[128,2560]{1,0:T(8,128)(2,1)S(1)} fusion(bf16[128,5120]{1,0:T(8,128)(2,1)} %param.6, s32[]{:T(128)S(6)} %select_n.16), kind=kLoop, calls=%fused_computation.2 | loop fusion | bytes 1310724 | tf_op jit(solution)/shard_map/dynamic_slice | solution.py:246
  10.2 8.0 %collective-permute-start.7 = (bf16[128,2560]{1,0:T(8,128)(2,1)S(1)}, bf16[128,2560]{1,0:T(8,128)(2,1)S(1)}, u32[]{:S(2)}, u32[]{:S(2)}) collective-permute-start(bf16[128,2560]{1,0:T(8,128)(2,1)S(1)} %constant_dynamic-slice_fusion.2.refs_1_.refs_7_), channel_id=1, source_target_pairs={{0,254},{1,255},{2,0},{3,1},{4,2},{5,3},{6,4},{7,5},{8,6},{9,7},{1... | collective-permute-start | bytes 1966088 | tf_op jit(solution)/shard_map/ppermute | solution.py:238
  18.2 1.2 %copy-done.3 = bf16[216,2560]{1,0:T(8,128)(2,1)S(1)} copy-done((bf16[216,2560]{1,0:T(8,128)(2,1)S(1)}, bf16[216,2560]{1,0:T(8,128)(2,1)}, u32[]{:S(2)}) %copy-start.3) | copy-done | bytes 1105944
  19.5 1.0 shard_map.84
  20.6 0.4 collective-permute-start
  21.0 11.5 %collective-permute-done.1.refs_0_.refs_8_ = bf16[128,2560]{1,0:T(8,128)(2,1)} collective-permute-done((bf16[128,2560]{1,0:T(8,128)(2,1)}, bf16[128,2560]{1,0:T(8,128)(2,1)}, u32[]{:S(2)}, u32[]{:S(2)}) %collective-permute-start.1) | collective-permute-done | bytes 655392 | tf_op jit(solution)/shard_map/ppermute | solution.py:238
  32.4 1.8 %shard_map.85 = (f32[2,216,128]{2,1,0:T(8,128)S(1)}, bf16[2,216,128]{2,1,0:T(8,128)(2,1)S(1)}) custom-call(bf16[128,2560]{1,0:T(8,128)(2,1)} %collective-permute-done.1.refs_0_.refs_8_, bf16[216,2560]{1,0:T(8,128)(2,1)S(1)} %copy-done.2, bf16[216,2560]{1,0:T(8,128)(2,1)S(1)} %copy-done.3), custom_call_target="tpu_custom_call" | custom-call | flops 283115520 | bytes 3198976 | tf_op jit(solution)/shard_map/pallas_call | solution.py:39
  34.3 2.3 %collective-permute-start.3 = (bf16[2,216,128]{2,1,0:T(8,128)(2,1)S(1)}, bf16[2,216,128]{2,1,0:T(8,128)(2,1)S(1)}, u32[]{:S(2)}, u32[]{:S(2)}) collective-permute-start(bf16[2,216,128]{2,1,0:T(8,128)(2,1)S(1)} %get-tuple-element.31), channel_id=1, source_target_pairs={{0,1},{1,0},{2,3},{3,2},{4,5},{5,4},{6,7},{7,6},{8,9},{9,8},{10,11... | collective-permute-start | bytes 331784 | tf_op jit(solution)/shard_map/ppermute | solution.py:238
  36.5 9.9 %collective-permute-done.2.refs_0_.refs_9_ = bf16[128,2560]{1,0:T(8,128)(2,1)} collective-permute-done((bf16[128,2560]{1,0:T(8,128)(2,1)}, bf16[128,2560]{1,0:T(8,128)(2,1)}, u32[]{:S(2)}, u32[]{:S(2)}) %collective-permute-start.2) | collective-permute-done | bytes 655392 | tf_op jit(solution)/shard_map/ppermute | solution.py:238
  46.5 1.5 %shard_map.86 = (f32[1,216,128]{2,1,0:T(8,128)S(1)}, bf16[1,216,128]{2,1,0:T(8,128)(2,1)S(1)}) custom-call(bf16[128,2560]{1,0:T(8,128)(2,1)} %collective-permute-done.2.refs_0_.refs_9_, bf16[216,2560]{1,0:T(8,128)(2,1)S(1)} %copy-done.1), custom_call_target="tpu_custom_call" | custom-call | flops 141557760 | bytes 1927168 | tf_op jit(solution)/shard_map/pallas_call | solution.py:39
  48.0 2.3 %collective-permute-start.4 = (bf16[1,216,128]{2,1,0:T(8,128)(2,1)S(1)}, bf16[1,216,128]{2,1,0:T(8,128)(2,1)S(1)}, u32[]{:S(2)}, u32[]{:S(2)}) collective-permute-start(bf16[1,216,128]{2,1,0:T(8,128)(2,1)S(1)} %get-tuple-element.32), channel_id=1, source_target_pairs={{0,1},{1,0},{2,3},{3,2},{4,5},{5,4},{6,7},{7,6},{8,9},{9,8},{10,11... | collective-permute-start | bytes 165896 | tf_op jit(solution)/shard_map/ppermute | solution.py:238
  50.3 3.9 %collective-permute-start.8 = (bf16[128,2560]{1,0:T(8,128)(2,1)}, bf16[128,2560]{1,0:T(8,128)(2,1)}, u32[]{:S(2)}, u32[]{:S(2)}) collective-permute-start(bf16[128,2560]{1,0:T(8,128)(2,1)} %constant_dynamic-slice_fusion.1), channel_id=1, source_target_pairs={{0,255},{1,254},{2,0},{3,1},{4,3},{5,2},{6,4},{7,5},{8,7},{9,6},{1... | collective-permute-start | bytes 1966088 | tf_op jit(solution)/shard_map/ppermute | solution.py:238
  54.2 0.1 collective-permute-start.9
  54.3 10.8 %collective-permute-start.10 = (bf16[128,2560]{1,0:T(8,128)(2,1)}, bf16[128,2560]{1,0:T(8,128)(2,1)}, u32[]{:S(2)}, u32[]{:S(2)}) collective-permute-start(bf16[128,2560]{1,0:T(8,128)(2,1)} %collective-permute-done.1.refs_0_.refs_8_), channel_id=1, source_target_pairs={{0,2},{1,3},{2,0},{3,1},{4,6},{5,7},{6,4},{7,5},{8,10},{9,11},{10,... | collective-permute-start | bytes 1966088 | tf_op jit(solution)/shard_map/ppermute | solution.py:238
  65.1 0.1 collective-permute-start.11
  65.2 2.6 %shard_map.87 = (bf16[3,216,256]{2,1,0:T(8,128)(2,1)S(1)}, f32[128,2560]{1,0:T(8,128)S(1)}, bf16[128,2560]{1,0:T(8,128)(2,1)}) custom-call(f32[3,216,128]{2,1,0:T(8,128)S(1)} %get-tuple-element.27.refs_0_, bf16[3,216,128]{2,1,0:T(8,128)(2,1)S(1)} %collective-permute-done.refs_1_, f32[2,216,128]{2,1,0:T(8,128)S(1)} %get-tuple-element.29.refs_2_, ...), custom_call_target="tpu_custom_call" | custom-call | flops 1132462080 | bytes 5505024 | tf_op jit(solution)/shard_map/pallas_call | solution.py:39
  67.7 1.1 copy-done.16
  68.8 0.7 copy-done.18
  69.5 0.9 copy-done.13
  70.4 0.4 collective-permute-start.5
  70.8 1.2 %copy-done.4 = bf16[216,2560]{1,0:T(8,128)(2,1)S(1)} copy-done((bf16[216,2560]{1,0:T(8,128)(2,1)S(1)}, bf16[216,2560]{1,0:T(8,128)(2,1)}, u32[]{:S(2)}) %copy-start.4) | copy-done | bytes 1105944
  72.0 1.1 copy-done.11
  73.1 1.1 copy-done.14
  74.2 1.0 shard_map.88
  75.3 0.1 collective-permute-start.13
  75.4 0.1 copy-done.5
  75.4 2.9 %shard_map.89 = (f32[3,216,128]{2,1,0:T(8,128)S(1)}, bf16[3,216,128]{2,1,0:T(8,128)(2,1)S(1)}) custom-call(s32[1]{0:T(128)} %bitcast.odd, bf16[128,2560]{1,0:T(8,128)(2,1)} %collective-permute-done.8.refs_0_, bf16[128,2560]{1,0:T(8,128)(2,1)} %collective-permute-done.9.refs_1_, bf16[128,2560]{1,0:T(8,128)(2,1)} %collective-permute-done.10.refs_2_, ...), custom_call_target="tpu_custom_call" | custom-call | flops 424673280 | bytes 6436868 | tf_op jit(solution)/shard_map/pallas_call | solution.py:39
  78.3 1.5 %collective-permute-start.12 = (bf16[3,216,128]{2,1,0:T(8,128)(2,1)S(1)}, bf16[3,216,128]{2,1,0:T(8,128)(2,1)S(1)}, u32[]{:S(2)}, u32[]{:S(2)}) collective-permute-start(bf16[3,216,128]{2,1,0:T(8,128)(2,1)S(1)} %get-tuple-element.37), channel_id=1, source_target_pairs={{0,1},{1,0},{2,3},{3,2},{4,5},{5,4},{6,7},{7,6},{8,9},{9,8},{10,11... | collective-permute-start | bytes 497672 | tf_op jit(solution)/shard_map/ppermute | solution.py:238
  79.8 1.2 %collective-permute-done.13.refs_5_ = bf16[3,216,128]{2,1,0:T(8,128)(2,1)S(1)} collective-permute-done((bf16[3,216,128]{2,1,0:T(8,128)(2,1)S(1)}, bf16[3,216,128]{2,1,0:T(8,128)(2,1)S(1)}, u32[]{:S(2)}, u32[]{:S(2)}) %collective-permute-start.13) | collective-permute-done | bytes 165920 | tf_op jit(solution)/shard_map/ppermute | solution.py:238
  81.1 3.6 %collective-permute-done.12.refs_4_ = bf16[3,216,128]{2,1,0:T(8,128)(2,1)S(1)} collective-permute-done((bf16[3,216,128]{2,1,0:T(8,128)(2,1)S(1)}, bf16[3,216,128]{2,1,0:T(8,128)(2,1)S(1)}, u32[]{:S(2)}, u32[]{:S(2)}) %collective-permute-start.12) | collective-permute-done | bytes 165920 | tf_op jit(solution)/shard_map/ppermute | solution.py:238
  84.7 3.0 %shard_map.90 = (bf16[3,216,256]{2,1,0:T(8,128)(2,1)S(1)}, bf16[128,2560]{1,0:T(8,128)(2,1)S(1)}, bf16[128,2560]{1,0:T(8,128)(2,1)S(1)}) custom-call(s32[1]{0:T(128)S(6)} %sub.8.refs_0_, bf16[128,2560]{1,0:T(8,128)(2,1)} %collective-permute-done.5.refs_1_, f32[3,216,128]{2,1,0:T(8,128)S(1)} %get-tuple-element.35.refs_2_, ...), custom_call_target="tpu_custom_call" | custom-call | flops 1132462080 | bytes 5505028 | tf_op jit(solution)/shard_map/pallas_call | solution.py:39
  87.7 0.1 collective-permute-start.14
  87.8 0.7 collective-permute-start.15
  88.5 0.1 collective-permute-start.16
  88.6 0.1 pad_add_fusion.where
  88.7 0.0 copy-start.17
  88.7 6.8 %shard_map.93 = (bf16[216,2560]{1,0:T(8,128)(2,1)}, bf16[216,2560]{1,0:T(8,128)(2,1)}, bf16[216,2560]{1,0:T(8,128)(2,1)}) custom-call(s32[1]{0:T(128)} %bitcast.odd, bf16[128,2560]{1,0:T(8,128)(2,1)} %collective-permute-done.8.refs_0_, bf16[128,2560]{1,0:T(8,128)(2,1)} %collective-permute-done.9.refs_1_, bf16[128,2560]{1,0:T(8,128)(2,1)} %collective-permute-done.10.refs_2_, ...), custom_call_target="tpu_custom_call" | custom-call | flops 1698693120 | bytes 10534916 | tf_op jit(solution)/shard_map/pallas_call | solution.py:39
  95.5 2.5 %collective-permute-done.14.b = bf16[128,2560]{1,0:T(8,128)(2,1)S(1)} collective-permute-done((bf16[128,2560]{1,0:T(8,128)(2,1)S(1)}, bf16[128,2560]{1,0:T(8,128)(2,1)S(1)}, u32[]{:S(2)}, u32[]{:S(2)}) %collective-permute-start.14) | collective-permute-done | bytes 655392 | tf_op jit(solution)/shard_map/ppermute | solution.py:238
  98.0 1.5 %shard_map.91._ = bf16[128,5120]{1,0:T(8,128)(2,1)} custom-call(s32[2]{0:T(128)S(1)} %pad_add_fusion.where, f32[128,2560]{1,0:T(8,128)S(1)} %copy-done.17, bf16[128,2560]{1,0:T(8,128)(2,1)S(1)} %collective-permute-done.14.b), custom_call_target="tpu_custom_call" | custom-call | tf_op jit(solution)/shard_map/pallas_call | solution.py:223
  99.6 11.1 %collective-permute-done.16.flip = bf16[128,2560]{1,0:T(8,128)(2,1)S(1)} collective-permute-done((bf16[128,2560]{1,0:T(8,128)(2,1)S(1)}, bf16[128,2560]{1,0:T(8,128)(2,1)S(1)}, u32[]{:S(2)}, u32[]{:S(2)}) %collective-permute-start.16) | collective-permute-done | bytes 655392 | tf_op jit(solution)/shard_map/ppermute | solution.py:238
  110.7 1.4 %shard_map.92 = bf16[128,5120]{1,0:T(8,128)(2,1)} custom-call(s32[2]{0:T(128)S(1)} %pad_add_fusion.where, bf16[128,5120]{1,0:T(8,128)(2,1)} %shard_map.91._, bf16[128,2560]{1,0:T(8,128)(2,1)S(1)} %collective-permute-done.15.left, bf16[128,2560]{1,0:T(8,128)(2,1)S(1)} %collective-permute-done.16.flip), custom_call_target="tpu_custom_call", output_to_operand_aliasing={{}: (1, {})} | custom-call | tf_op jit(solution)/shard_map/pallas_call | solution.py:223
  (43 shorter events, 0.1 us)
Async XLA Ops:
  0.6 1.3 %copy-start = (bf16[128,5120]{1,0:T(8,128)(2,1)S(1)}, bf16[128,5120]{1,0:T(8,128)(2,1)}, u32[]{:S(2)}) copy-start(bf16[128,5120]{1,0:T(8,128)(2,1)} %param.5) | copy-start | bytes 3932164
  0.6 4.2 %copy-start.20 = (bf16[128,5120]{1,0:T(8,128)(2,1)S(1)}, bf16[128,5120]{1,0:T(8,128)(2,1)}, u32[]{:S(2)}) copy-start(bf16[128,5120]{1,0:T(8,128)(2,1)} %param.6) | copy-start | bytes 3932164
  2.8 29.6 %collective-permute-start.1 = (bf16[128,2560]{1,0:T(8,128)(2,1)}, bf16[128,2560]{1,0:T(8,128)(2,1)}, u32[]{:S(2)}, u32[]{:S(2)}) collective-permute-start(bf16[128,2560]{1,0:T(8,128)(2,1)} %constant_dynamic-slice_fusion.1), channel_id=1, source_target_pairs={{0,1},{1,0},{2,3},{3,2},{4,5},{5,4},{6,7},{7,6},{8,9},{9,8},{10,11... | collective-permute-start | bytes 1966088 | tf_op jit(solution)/shard_map/ppermute | solution.py:238
  5.7 40.7 %collective-permute-start.2 = (bf16[128,2560]{1,0:T(8,128)(2,1)}, bf16[128,2560]{1,0:T(8,128)(2,1)}, u32[]{:S(2)}, u32[]{:S(2)}) collective-permute-start(bf16[128,2560]{1,0:T(8,128)(2,1)} %constant_dynamic-slice_fusion), channel_id=1, source_target_pairs={{0,1},{1,0},{2,3},{3,2},{4,5},{5,4},{6,7},{7,6},{8,9},{9,8},{10,11... | collective-permute-start | bytes 1966088 | tf_op jit(solution)/shard_map/ppermute | solution.py:238
  5.7 12.5 %copy-start.1 = (bf16[216,2560]{1,0:T(8,128)(2,1)S(1)}, bf16[216,2560]{1,0:T(8,128)(2,1)}, u32[]{:S(2)}) copy-start(bf16[216,2560]{1,0:T(8,128)(2,1)} %refs_6_.4) | copy-start | bytes 3317764
  5.7 12.5 %copy-start.2 = (bf16[216,2560]{1,0:T(8,128)(2,1)S(1)}, bf16[216,2560]{1,0:T(8,128)(2,1)}, u32[]{:S(2)}) copy-start(bf16[216,2560]{1,0:T(8,128)(2,1)} %refs_6_.5) | copy-start | bytes 3317764
  5.8 14.7 %copy-start.6 = (bf16[128,2560]{1,0:T(8,128)(2,1)}, bf16[128,2560]{1,0:T(8,128)(2,1)S(1)}, u32[]{:S(2)}) copy-start(bf16[128,2560]{1,0:T(8,128)(2,1)S(1)} %constant_dynamic-slice_fusion.3.refs_0_.refs_6_) | copy-start | bytes 1966084
  5.8 48.4 %collective-permute-start.6 = (bf16[128,2560]{1,0:T(8,128)(2,1)S(1)}, bf16[128,2560]{1,0:T(8,128)(2,1)S(1)}, u32[]{:S(2)}, u32[]{:S(2)}) collective-permute-start(bf16[128,2560]{1,0:T(8,128)(2,1)S(1)} %constant_dynamic-slice_fusion.3.refs_0_.refs_6_), channel_id=1, source_target_pairs={{0,254},{1,255},{2,0},{3,1},{4,2},{5,3},{6,4},{7,5},{8,6},{9,7},{1... | collective-permute-start | bytes 1966088 | tf_op jit(solution)/shard_map/ppermute | solution.py:238
  10.2 10.3 %copy-start.8 = (bf16[128,2560]{1,0:T(8,128)(2,1)}, bf16[128,2560]{1,0:T(8,128)(2,1)S(1)}, u32[]{:S(2)}) copy-start(bf16[128,2560]{1,0:T(8,128)(2,1)S(1)} %constant_dynamic-slice_fusion.2.refs_1_.refs_7_) | copy-start | bytes 1966084
  10.2 59.3 %collective-permute-start.7 = (bf16[128,2560]{1,0:T(8,128)(2,1)S(1)}, bf16[128,2560]{1,0:T(8,128)(2,1)S(1)}, u32[]{:S(2)}, u32[]{:S(2)}) collective-permute-start(bf16[128,2560]{1,0:T(8,128)(2,1)S(1)} %constant_dynamic-slice_fusion.2.refs_1_.refs_7_), channel_id=1, source_target_pairs={{0,254},{1,255},{2,0},{3,1},{4,2},{5,3},{6,4},{7,5},{8,6},{9,7},{1... | collective-permute-start | bytes 1966088 | tf_op jit(solution)/shard_map/ppermute | solution.py:238
  18.2 1.2 %copy-start.3 = (bf16[216,2560]{1,0:T(8,128)(2,1)S(1)}, bf16[216,2560]{1,0:T(8,128)(2,1)}, u32[]{:S(2)}) copy-start(bf16[216,2560]{1,0:T(8,128)(2,1)} %refs_7_.3) | copy-start | bytes 3317764
  20.6 29.7 %collective-permute-start = (bf16[3,216,128]{2,1,0:T(8,128)(2,1)S(1)}, bf16[3,216,128]{2,1,0:T(8,128)(2,1)S(1)}, u32[]{:S(2)}, u32[]{:S(2)}) collective-permute-start(bf16[3,216,128]{2,1,0:T(8,128)(2,1)S(1)} %get-tuple-element.28), channel_id=1, source_target_pairs={{0,1},{1,0},{2,3},{3,2},{4,5},{5,4},{6,7},{7,6},{8,9},{9,8},{10,11... | collective-permute-start | bytes 497672 | tf_op jit(solution)/shard_map/ppermute | solution.py:238
  34.3 30.8 %collective-permute-start.3 = (bf16[2,216,128]{2,1,0:T(8,128)(2,1)S(1)}, bf16[2,216,128]{2,1,0:T(8,128)(2,1)S(1)}, u32[]{:S(2)}, u32[]{:S(2)}) collective-permute-start(bf16[2,216,128]{2,1,0:T(8,128)(2,1)S(1)} %get-tuple-element.31), channel_id=1, source_target_pairs={{0,1},{1,0},{2,3},{3,2},{4,5},{5,4},{6,7},{7,6},{8,9},{9,8},{10,11... | collective-permute-start | bytes 331784 | tf_op jit(solution)/shard_map/ppermute | solution.py:238
  48.0 6.3 %collective-permute-start.4 = (bf16[1,216,128]{2,1,0:T(8,128)(2,1)S(1)}, bf16[1,216,128]{2,1,0:T(8,128)(2,1)S(1)}, u32[]{:S(2)}, u32[]{:S(2)}) collective-permute-start(bf16[1,216,128]{2,1,0:T(8,128)(2,1)S(1)} %get-tuple-element.32), channel_id=1, source_target_pairs={{0,1},{1,0},{2,3},{3,2},{4,5},{5,4},{6,7},{7,6},{8,9},{9,8},{10,11... | collective-permute-start | bytes 165896 | tf_op jit(solution)/shard_map/ppermute | solution.py:238
  50.3 25.0 %collective-permute-start.8 = (bf16[128,2560]{1,0:T(8,128)(2,1)}, bf16[128,2560]{1,0:T(8,128)(2,1)}, u32[]{:S(2)}, u32[]{:S(2)}) collective-permute-start(bf16[128,2560]{1,0:T(8,128)(2,1)} %constant_dynamic-slice_fusion.1), channel_id=1, source_target_pairs={{0,255},{1,254},{2,0},{3,1},{4,3},{5,2},{6,4},{7,5},{8,7},{9,6},{1... | collective-permute-start | bytes 1966088 | tf_op jit(solution)/shard_map/ppermute | solution.py:238
  54.2 13.5 %copy-start.10 = (bf16[128,2560]{1,0:T(8,128)(2,1)}, bf16[128,2560]{1,0:T(8,128)(2,1)S(1)}, u32[]{:S(2)}) copy-start(bf16[128,2560]{1,0:T(8,128)(2,1)S(1)} %collective-permute-done.6.refs_0_.refs_10_) | copy-start | bytes 1966084
  54.2 21.2 %collective-permute-start.9 = (bf16[128,2560]{1,0:T(8,128)(2,1)}, bf16[128,2560]{1,0:T(8,128)(2,1)}, u32[]{:S(2)}, u32[]{:S(2)}) collective-permute-start(bf16[128,2560]{1,0:T(8,128)(2,1)} %constant_dynamic-slice_fusion), channel_id=1, source_target_pairs={{0,255},{1,254},{2,0},{3,1},{4,3},{5,2},{6,4},{7,5},{8,7},{9,6},{1... | collective-permute-start | bytes 1966088 | tf_op jit(solution)/shard_map/ppermute | solution.py:238
  54.3 21.1 %collective-permute-start.10 = (bf16[128,2560]{1,0:T(8,128)(2,1)}, bf16[128,2560]{1,0:T(8,128)(2,1)}, u32[]{:S(2)}, u32[]{:S(2)}) collective-permute-start(bf16[128,2560]{1,0:T(8,128)(2,1)} %collective-permute-done.1.refs_0_.refs_8_), channel_id=1, source_target_pairs={{0,2},{1,3},{2,0},{3,1},{4,6},{5,7},{6,4},{7,5},{8,10},{9,11},{10,... | collective-permute-start | bytes 1966088 | tf_op jit(solution)/shard_map/ppermute | solution.py:238
  65.1 10.3 %collective-permute-start.11 = (bf16[128,2560]{1,0:T(8,128)(2,1)}, bf16[128,2560]{1,0:T(8,128)(2,1)}, u32[]{:S(2)}, u32[]{:S(2)}) collective-permute-start(bf16[128,2560]{1,0:T(8,128)(2,1)} %collective-permute-done.2.refs_0_.refs_9_), channel_id=1, source_target_pairs={{0,2},{1,3},{2,0},{3,1},{4,6},{5,7},{6,4},{7,5},{8,10},{9,11},{10,... | collective-permute-start | bytes 1966088 | tf_op jit(solution)/shard_map/ppermute | solution.py:238
  67.7 1.1 copy-start.16
  68.8 0.7 copy-start.18
  69.5 0.9 copy-start.13
  70.4 10.7 %collective-permute-start.5 = (bf16[128,2560]{1,0:T(8,128)(2,1)}, bf16[128,2560]{1,0:T(8,128)(2,1)}, u32[]{:S(2)}, u32[]{:S(2)}) collective-permute-start(bf16[128,2560]{1,0:T(8,128)(2,1)} %get-tuple-element.34), channel_id=1, source_target_pairs={{0,2},{1,3},{2,0},{3,1},{4,6},{5,7},{6,4},{7,5},{8,10},{9,11},{10,... | collective-permute-start | bytes 1966088 | tf_op jit(solution)/shard_map/ppermute | solution.py:238
  70.8 1.2 %copy-start.4 = (bf16[216,2560]{1,0:T(8,128)(2,1)S(1)}, bf16[216,2560]{1,0:T(8,128)(2,1)}, u32[]{:S(2)}) copy-start(bf16[216,2560]{1,0:T(8,128)(2,1)} %refs_7_.3) | copy-start | bytes 3317764
  72.0 1.1 copy-start.11
  73.1 1.1 copy-start.14
  74.2 1.2 %copy-start.5 = (bf16[216,2560]{1,0:T(8,128)(2,1)S(1)}, bf16[216,2560]{1,0:T(8,128)(2,1)}, u32[]{:S(2)}) copy-start(bf16[216,2560]{1,0:T(8,128)(2,1)} %refs_7_.3) | copy-start | bytes 3317764
  75.3 5.8 %collective-permute-start.13 = (bf16[3,216,128]{2,1,0:T(8,128)(2,1)S(1)}, bf16[3,216,128]{2,1,0:T(8,128)(2,1)S(1)}, u32[]{:S(2)}, u32[]{:S(2)}) collective-permute-start(bf16[3,216,128]{2,1,0:T(8,128)(2,1)S(1)} %get-tuple-element.38), channel_id=1, source_target_pairs={{0,1},{1,0},{2,3},{3,2},{4,5},{5,4},{6,7},{7,6},{8,9},{9,8},{10,11... | collective-permute-start | bytes 497672 | tf_op jit(solution)/shard_map/ppermute | solution.py:238
  78.3 6.3 %collective-permute-start.12 = (bf16[3,216,128]{2,1,0:T(8,128)(2,1)S(1)}, bf16[3,216,128]{2,1,0:T(8,128)(2,1)S(1)}, u32[]{:S(2)}, u32[]{:S(2)}) collective-permute-start(bf16[3,216,128]{2,1,0:T(8,128)(2,1)S(1)} %get-tuple-element.37), channel_id=1, source_target_pairs={{0,1},{1,0},{2,3},{3,2},{4,5},{5,4},{6,7},{7,6},{8,9},{9,8},{10,11... | collective-permute-start | bytes 497672 | tf_op jit(solution)/shard_map/ppermute | solution.py:238
  84.7 4.0 %copy-start.7 = (bf16[128,2560]{1,0:T(8,128)(2,1)S(1)}, bf16[128,2560]{1,0:T(8,128)(2,1)}, u32[]{:S(2)}) copy-start(bf16[128,2560]{1,0:T(8,128)(2,1)} %copy-done.6) | copy-start | bytes 1966084
  84.7 4.0 %copy-start.9 = (bf16[128,2560]{1,0:T(8,128)(2,1)S(1)}, bf16[128,2560]{1,0:T(8,128)(2,1)}, u32[]{:S(2)}) copy-start(bf16[128,2560]{1,0:T(8,128)(2,1)} %copy-done.8) | copy-start | bytes 1966084
  84.7 4.0 %copy-start.12 = (bf16[128,2560]{1,0:T(8,128)(2,1)S(1)}, bf16[128,2560]{1,0:T(8,128)(2,1)}, u32[]{:S(2)}) copy-start(bf16[128,2560]{1,0:T(8,128)(2,1)} %copy-done.10) | copy-start | bytes 1966084
  84.7 4.0 %copy-start.15 = (bf16[128,2560]{1,0:T(8,128)(2,1)S(1)}, bf16[128,2560]{1,0:T(8,128)(2,1)}, u32[]{:S(2)}) copy-start(bf16[128,2560]{1,0:T(8,128)(2,1)} %copy-done.13) | copy-start | bytes 1966084
  84.7 4.0 %copy-start.19 = (bf16[3,216,256]{2,1,0:T(8,128)(2,1)S(1)}, bf16[3,216,256]{2,1,0:T(8,128)(2,1)}, u32[]{:S(2)}) copy-start(bf16[3,216,256]{2,1,0:T(8,128)(2,1)} %copy-done.18) | copy-start | bytes 995332
  87.7 10.4 %collective-permute-start.14 = (bf16[128,2560]{1,0:T(8,128)(2,1)S(1)}, bf16[128,2560]{1,0:T(8,128)(2,1)S(1)}, u32[]{:S(2)}, u32[]{:S(2)}) collective-permute-start(bf16[128,2560]{1,0:T(8,128)(2,1)S(1)} %get-tuple-element.39), channel_id=1, source_target_pairs={{0,2},{1,3},{2,4},{3,5},{4,6},{5,7},{6,8},{7,9},{8,10},{9,11},{10,... | collective-permute-start | bytes 1966088 | tf_op jit(solution)/shard_map/ppermute | solution.py:238
  87.8 11.8 %collective-permute-start.15 = (bf16[128,2560]{1,0:T(8,128)(2,1)}, bf16[128,2560]{1,0:T(8,128)(2,1)S(1)}, u32[]{:S(2)}, u32[]{:S(2)}) collective-permute-start(bf16[128,2560]{1,0:T(8,128)(2,1)} %get-tuple-element.34), channel_id=1, source_target_pairs={{0,1},{1,0},{4,5},{5,4},{8,9},{9,8},{12,13},{13,12},{16,17},{17,16... | collective-permute-start | bytes 1966088 | tf_op jit(solution)/shard_map/ppermute | solution.py:238
  88.5 22.2 %collective-permute-start.16 = (bf16[128,2560]{1,0:T(8,128)(2,1)S(1)}, bf16[128,2560]{1,0:T(8,128)(2,1)S(1)}, u32[]{:S(2)}, u32[]{:S(2)}) collective-permute-start(bf16[128,2560]{1,0:T(8,128)(2,1)S(1)} %get-tuple-element.40), channel_id=1, source_target_pairs={{0,3},{1,2},{2,5},{3,4},{4,7},{5,6},{6,9},{7,8},{8,11},{9,10},{10,... | collective-permute-start | bytes 1966088 | tf_op jit(solution)/shard_map/ppermute | solution.py:238
  88.7 9.4 %copy-start.17 = (f32[128,2560]{1,0:T(8,128)S(1)}, f32[128,2560]{1,0:T(8,128)}, u32[]{:S(2)}) copy-start(f32[128,2560]{1,0:T(8,128)} %copy-done.16) | copy-start | bytes 3932164
